TPU v7x, 512 devices: a whole 4x4x16 slice. The times are simulated.
512 devices in a mesh: var: 32 (over z_lo, y, core), head: 16 (over z_hi, x).
Axes of the slice: x: 4, y: 4, z: 16 (z_hi: 4, z_lo: 4; z = z_hi * 4 + z_lo), core: 2. Of those that a mesh axis runs over, the one named last changes fastest.
Arguments:
- queries: bfloat16 [16384, 8192], P('var', 'head'), may hold values from -5 to 5
- ablated: int32 [16384], P('var'), may hold values from 0 to 63
- head_keep: int32 [32, 64], P(None, 'head'), may hold values 0 or 1
- k_cache: bfloat16 [32, 2048, 1024], P('var', 'head'), may hold values from -4 to 4
- v_cache: bfloat16 [32, 2048, 1024], P('var', 'head'), may hold values from -40 to 40
- lengths: int32 [32], P('var'), may hold values from 512 to 2048, as said below
- out_weight: bfloat16 [8192, 4096], P('head', 'var'), may hold values from -0.125 to 0.125
- residual: bfloat16 [16384, 4096], P('var', 'head'), may hold values from -6 to 6
Outputs:
- patched: bfloat16 [16384, 4096], P('var', 'head')
Inputs may be any that keep to these rules, and one draw needn't show every extreme that they name: `lengths`: one prompt has exactly 2048 live positions.
All inputs are finite; a program needn't handle non-finite values. No bound on the sum of `head_keep` on one device may be relied on, other than what follows from the above.
Results may differ from a plain program's by a relative error of at most 0.012.
Values may be sent and summed in bfloat16 or wider, within the bound.
No kernel may reach another device: no remote copies, remote signals or barrier semaphores. Data moves between devices by JAX's collectives and lax.ppermute only.
A program may use at most 64 MiB of HBM per device.

v0:
```python
import math

import jax
import jax.numpy as jnp
from jax import lax
from jax.experimental import pallas as pl
from jax.experimental.pallas import tpu as pltpu
from jax.sharding import Mesh, PartitionSpec as P


HD = 128
VAR = ("zl", "y", "c")
HEAD = ("zh", "x")
ROW_BLOCK = 128


def attend_kernel(info, q_ref, *refs):
    kv, (out_ref, k_all, v_all) = refs[:-3], refs[-3:]
    slots, _, span, _ = kv[0].shape
    base = 1 + q_ref.shape[1] // HD

    @pl.when(pl.program_id(0) == 0)
    def _():
        for t, kv_ref in enumerate(kv):
            for s in range(slots):
                at = pl.ds(pl.multiple_of(info[base + t * slots + s] * span, span), span)
                k_all[at, :] = kv_ref[s, 0]
                v_all[at, :] = kv_ref[s, 1]

    positions = k_all.shape[0]
    live = lax.broadcasted_iota(jnp.int32, (1, positions), 1) < info[0]
    bias = jnp.where(live, 0.0, -jnp.inf).astype(jnp.float32)
    scale = math.log2(math.e) / math.sqrt(HD)
    for j in range(q_ref.shape[1] // HD):
        cols = slice(j * HD, (j + 1) * HD)
        scores = lax.dot_general(
            q_ref[:, cols], k_all[...], (((1,), (1,)), ((), ())), preferred_element_type=jnp.float32
        )
        scores = scores * scale + bias
        top = jnp.max(scores, axis=-1, keepdims=True)
        weight = jnp.exp2(scores - top)
        total = jnp.sum(weight, axis=-1, keepdims=True)
        mixed = jnp.dot(weight.astype(jnp.bfloat16), v_all[...], preferred_element_type=jnp.float32)
        first = q_ref[:, j * HD : j * HD + 1].astype(jnp.float32)
        keep = jnp.logical_and(first != jnp.inf, info[1 + j] != 0)
        out_ref[:, cols] = jnp.where(keep, mixed / total, 0.0).astype(jnp.bfloat16)


def attend(info, queries, kv):
    rows, feats = queries.shape
    slots, _, span, _ = kv[0].shape
    positions = len(kv) * slots * span
    return pl.pallas_call(
        attend_kernel,
        out_shape=jax.ShapeDtypeStruct((rows, feats), jnp.bfloat16),
        grid_spec=pltpu.PrefetchScalarGridSpec(
            num_scalar_prefetch=1,
            grid=(rows // ROW_BLOCK,),
            in_specs=[pl.BlockSpec((ROW_BLOCK, feats), lambda i, s: (i, 0))]
            + [pl.BlockSpec(kv[0].shape, lambda i, s: (0, 0, 0, 0))] * len(kv),
            out_specs=pl.BlockSpec((ROW_BLOCK, feats), lambda i, s: (i, 0)),
            scratch_shapes=[
                pltpu.VMEM((positions, HD), jnp.bfloat16),
                pltpu.VMEM((positions, HD), jnp.bfloat16),
            ],
        ),
        cost_estimate=pl.CostEstimate(
            flops=4 * rows * feats * positions,
            transcendentals=rows * (feats // HD) * positions,
            bytes_accessed=4 * rows * feats + 4 * positions * HD,
        ),
        compiler_params=pltpu.CompilerParams(vmem_limit_bytes=40 << 20),
        name="attend",
    )(info, queries, *kv)


def place_kernel(where, *refs):
    parts, out_ref = refs[:-1], refs[-1]
    for t, part in enumerate(parts):
        for s in range(4):
            out_ref[where[t], :, pl.ds(pl.multiple_of(where[4 + s] * 128, 128), 128)] = part[s]


def place(where, parts):
    spec = pl.BlockSpec(memory_space=pltpu.VMEM)
    return pl.pallas_call(
        place_kernel,
        out_shape=jax.ShapeDtypeStruct((4, 512, 512), jnp.bfloat16),
        in_specs=[pl.BlockSpec(memory_space=pltpu.SMEM)] + [spec] * len(parts),
        out_specs=spec,
        cost_estimate=pl.CostEstimate(flops=0, transcendentals=0, bytes_accessed=4 << 20),
        compiler_params=pltpu.CompilerParams(vmem_limit_bytes=16 << 20),
        name="place",
    )(where, *parts)


def project_kernel(where, *refs):
    gated, (own_ref, other_ref, out_ref) = refs[:-3], refs[-3:]
    c = where[0]
    for u, w_ref in enumerate((own_ref, other_ref)):
        lanes = pl.ds(pl.multiple_of((c if u == 0 else 1 - c) * 128, 128), 128)
        for pair in range(2):
            total = None
            for s, g_ref in enumerate(gated):
                term = jnp.dot(
                    g_ref[...],
                    w_ref[where[1 + s], :, pair * 256 : (pair + 1) * 256],
                    preferred_element_type=jnp.float32,
                )
                total = term if total is None else total + term
            total = total.astype(jnp.bfloat16)
            out_ref[2 * pair, :, lanes] = total[:, :128]
            out_ref[2 * pair + 1, :, lanes] = total[:, 128:]


def project(where, gated, own, other):
    parts = len(gated)
    rows, feats = gated[0].shape
    spec = pl.BlockSpec(memory_space=pltpu.VMEM)
    return pl.pallas_call(
        project_kernel,
        out_shape=jax.ShapeDtypeStruct((4, rows, 256), jnp.bfloat16),
        in_specs=[pl.BlockSpec(memory_space=pltpu.SMEM)] + [spec] * (parts + 2),
        out_specs=spec,
        cost_estimate=pl.CostEstimate(
            flops=2 * parts * rows * feats * 1024, transcendentals=0, bytes_accessed=8 << 20
        ),
        compiler_params=pltpu.CompilerParams(vmem_limit_bytes=24 << 20),
        name="project",
    )(where, *gated, own, other)


def shifted(size, by):
    return [(i, (i + by) % size) for i in range(size)]


def gather_weight(out_weight, y, zl):
    turned = lax.ppermute(out_weight, ("y", "x"), [(y * 4 + x, x * 4 + y) for y in range(4) for x in range(4)])
    along = [turned]
    for s in (1, 2, 3):
        along.append(lax.ppermute(turned, "zl", shifted(4, s)))
    along = jnp.stack(along)
    parts = [along]
    for s in (1, 2, 3):
        parts.append(lax.ppermute(along, "y", shifted(4, s)))
    where = jnp.stack([(y + 4 - t) & 3 for t in range(4)] + [(zl + 4 - s) & 3 for s in range(4)])
    own = place(where.astype(jnp.int32), parts)
    other = lax.ppermute(own, "c", [(0, 1), (1, 0)])
    return own, other


def step(queries, ablated, head_keep, k_cache, v_cache, lengths, out_weight, residual):
    row_count, feature_count = queries.shape
    prompts, local_heads = head_keep.shape
    per_prompt = row_count // prompts
    var_position = lax.axis_index(VAR)
    head_position = lax.axis_index(HEAD)
    x = lax.axis_index("x")
    first_head = head_position * local_heads

    zh = lax.axis_index("zh")
    caches = jnp.stack([k_cache[0], v_cache[0]])

    def heads_for(other_zh):
        return lax.dynamic_slice_in_dim(caches, other_zh * (2 * HD), 2 * HD, 2)

    kv = [heads_for(zh)]
    for s in (1, 2, 3):
        kv.append(lax.ppermute(heads_for((zh + s) & 3), "zh", shifted(4, s)))
    kv = jnp.stack(kv)

    def head_for(other_x):
        return lax.dynamic_slice_in_dim(kv, (other_x >> 1) * HD, HD, 3)

    kv_here = [head_for(x)]
    for t in (1, 2, 3):
        kv_here.append(lax.ppermute(head_for((x + t) & 3), "x", shifted(4, t)))
    block_of = [((zh - s) & 3) * 4 + ((x - t) & 3) for t in range(4) for s in range(4)]

    own, other = gather_weight(out_weight, lax.axis_index("y"), lax.axis_index("zl"))

    head_of = first_head + lax.broadcasted_iota(jnp.int32, (1, feature_count), 1) // HD
    marked = jnp.where(ablated[:, None] == head_of, jnp.inf, queries).astype(queries.dtype)
    arrived = lax.all_to_all(
        marked.reshape(prompts, per_prompt, feature_count), VAR, 0, 0, tiled=True
    ).reshape(row_count, feature_count)

    keep = lax.dynamic_index_in_dim(head_keep, var_position, 0, keepdims=False)
    gated = attend(jnp.concatenate([lengths, keep, jnp.stack(block_of)]), arrived, kv_here)

    gathered = [gated]
    for s in (1, 2, 3):
        gathered.append(lax.ppermute(gated, "x", shifted(4, s)))
    where = jnp.stack([lax.axis_index("c")] + [(x + 4 - s) & 3 for s in range(4)]).astype(jnp.int32)
    partial = project(where, gathered, own, other)
    partial = partial.reshape(4 * prompts, per_prompt, 256)
    returned = lax.all_to_all(partial, ("zh",) + VAR, 0, 0, tiled=True)
    projected = jnp.sum(returned.reshape(4, row_count, 256).astype(jnp.float32), axis=0)
    projected = projected.astype(jnp.bfloat16)
    return (residual.astype(jnp.float32) + projected.astype(jnp.float32)).astype(jnp.bfloat16)


def solution(mesh):
    split = Mesh(mesh.devices.reshape(4, 4, 2, 4, 4), VAR + HEAD)
    return jax.shard_map(
        step,
        mesh=split,
        in_specs=(
            P(VAR, HEAD),
            P(VAR),
            P(None, HEAD),
            P(VAR, HEAD, None),
            P(VAR, HEAD, None),
            P(VAR),
            P(HEAD, VAR),
            P(VAR, HEAD),
        ),
        out_specs=P(VAR, HEAD),
        check_vma=False,
    )
```

profile of v0, /device:TPU:33, one launch (start us, length us, event | category | flops | bytes accessed | tf_op | source)
XLA Modules:
  0.0 253.7 jit_solution(454841938481723857)
XLA Ops:
  0.0 1.7 collective-permute-start.9
  1.7 1.9 collective-permute-start.12
  3.6 4.9 %collective-permute-start.11 = (bf16[512,128]{1,0:T(8,128)(2,1)S(1)}, bf16[512,128]{1,0:T(8,128)(2,1)S(1)}, u32[]{:S(2)}, u32[]{:S(2)}) collective-permute-start(bf16[512,128]{1,0:T(8,128)(2,1)S(1)} %collective-permute-done.9), channel_id=1, source_target_pairs={{0,256},{128,384},{256,0},{384,128},{1,257},{129,385},{257,1},{385... | collective-permute-start | bytes 393224 | tf_op jit(solution)/shard_map/ppermute | solution.py:141
  8.5 4.3 %collective-permute-start.10 = (bf16[512,128]{1,0:T(8,128)(2,1)S(1)}, bf16[512,128]{1,0:T(8,128)(2,1)S(1)}, u32[]{:S(2)}, u32[]{:S(2)}) collective-permute-start(bf16[512,128]{1,0:T(8,128)(2,1)S(1)} %collective-permute-done.9), channel_id=1, source_target_pairs={{0,128},{128,256},{256,384},{384,0},{1,129},{129,257},{257,385},{3... | collective-permute-start | bytes 393224 | tf_op jit(solution)/shard_map/ppermute | solution.py:141
  12.8 2.0 compare_select_fusion
  14.8 19.3 %all-to-all-start = ((bf16[32,16,512]{2,1,0:T(8,128)(2,1)}), bf16[32,16,512]{2,1,0:T(8,128)(2,1)}, u32[]{:S(2)}, u32[]{:S(2)}) async-start(bf16[32,16,512]{2,1,0:T(8,128)(2,1)} %bitcast.21), calls=%async_computation | async-start | bytes 1048576 | tf_op jit(solution)/shard_map/all_to_all | solution.py:184
  34.3 4.3 %collective-permute-start.15 = (bf16[4,512,128]{2,1,0:T(8,128)(2,1)S(1)}, bf16[4,512,128]{2,1,0:T(8,128)(2,1)S(1)}, u32[]{:S(2)}, u32[]{:S(2)}) collective-permute-start(bf16[4,512,128]{2,1,0:T(8,128)(2,1)S(1)} %pad_maximum_fusion.1.refs_0_), channel_id=1, source_target_pairs={{0,96},{32,0},{64,32},{96,64},{1,97},{33,1},{65,33},{97,65},{2,98}... | collective-permute-start | bytes 1572872 | tf_op jit(solution)/shard_map/ppermute | solution.py:145
  38.6 2.5 collective-permute-start.14
  41.1 2.5 collective-permute-start.13
  43.7 9.6 %collective-permute-done.15.refs_3_ = bf16[4,512,128]{2,1,0:T(8,128)(2,1)S(1)} collective-permute-done((bf16[4,512,128]{2,1,0:T(8,128)(2,1)S(1)}, bf16[4,512,128]{2,1,0:T(8,128)(2,1)S(1)}, u32[]{:S(2)}, u32[]{:S(2)}) %collective-permute-start.15) | collective-permute-done | bytes 524320 | tf_op jit(solution)/shard_map/ppermute | solution.py:145
  53.3 3.8 %collective-permute-done.14.refs_2_ = bf16[4,512,128]{2,1,0:T(8,128)(2,1)S(1)} collective-permute-done((bf16[4,512,128]{2,1,0:T(8,128)(2,1)S(1)}, bf16[4,512,128]{2,1,0:T(8,128)(2,1)S(1)}, u32[]{:S(2)}, u32[]{:S(2)}) %collective-permute-start.14) | collective-permute-done | bytes 524320 | tf_op jit(solution)/shard_map/ppermute | solution.py:145
  57.1 0.8 copy-done.1
  57.9 11.0 %collective-permute-done.13.refs_1_ = bf16[4,512,128]{2,1,0:T(8,128)(2,1)S(1)} collective-permute-done((bf16[4,512,128]{2,1,0:T(8,128)(2,1)S(1)}, bf16[4,512,128]{2,1,0:T(8,128)(2,1)S(1)}, u32[]{:S(2)}, u32[]{:S(2)}) %collective-permute-start.13) | collective-permute-done | bytes 524320 | tf_op jit(solution)/shard_map/ppermute | solution.py:145
  68.9 0.8 copy-done.3
  69.7 1.0 copy-done.2
  70.7 1.0 copy-done.4
  71.7 0.9 place.1.refs_4_
  72.7 2.3 collective-permute-start.16
  75.0 1.0 constant_dynamic-update-slice_fusion
  76.1 10.3 %collective-permute-start.2 = (bf16[2,128,256]{2,1,0:T(8,128)(2,1)S(1)}, bf16[2,128,256]{2,1,0:T(8,128)(2,1)S(1)}, u32[]{:S(2)}, u32[]{:S(2)}) collective-permute-start(bf16[2,128,256]{2,1,0:T(8,128)(2,1)S(1)} %get-tuple-element.10), channel_id=1, source_target_pairs={{0,12},{4,0},{8,4},{12,8},{1,13},{5,1},{9,5},{13,9},{2,14},{6,2},{... | collective-permute-start | bytes 393224 | tf_op jit(solution)/shard_map/ppermute | solution.py:169
  86.4 5.5 %collective-permute-start.1 = (bf16[2,128,256]{2,1,0:T(8,128)(2,1)S(1)}, bf16[2,128,256]{2,1,0:T(8,128)(2,1)S(1)}, u32[]{:S(2)}, u32[]{:S(2)}) collective-permute-start(bf16[2,128,256]{2,1,0:T(8,128)(2,1)S(1)} %get-tuple-element.11), channel_id=1, source_target_pairs={{0,8},{4,12},{8,0},{12,4},{1,9},{5,13},{9,1},{13,5},{2,10},{6,14},... | collective-permute-start | bytes 393224 | tf_op jit(solution)/shard_map/ppermute | solution.py:169
  91.9 6.7 %collective-permute-start = (bf16[2,128,256]{2,1,0:T(8,128)(2,1)S(1)}, bf16[2,128,256]{2,1,0:T(8,128)(2,1)S(1)}, u32[]{:S(2)}, u32[]{:S(2)}) collective-permute-start(bf16[2,128,256]{2,1,0:T(8,128)(2,1)S(1)} %get-tuple-element.12), channel_id=1, source_target_pairs={{0,4},{4,8},{8,12},{12,0},{1,5},{5,9},{9,13},{13,1},{2,6},{6,10},{... | collective-permute-start | bytes 393224 | tf_op jit(solution)/shard_map/ppermute | solution.py:169
  98.6 13.7 %collective-permute-done.1 = bf16[2,128,256]{2,1,0:T(8,128)(2,1)S(1)} collective-permute-done((bf16[2,128,256]{2,1,0:T(8,128)(2,1)S(1)}, bf16[2,128,256]{2,1,0:T(8,128)(2,1)S(1)}, u32[]{:S(2)}, u32[]{:S(2)}) %collective-permute-start.1) | collective-permute-done | bytes 131104 | tf_op jit(solution)/shard_map/ppermute | solution.py:169
  112.3 1.0 constant_dynamic-slice_fusion
  113.3 1.9 collective-permute-start.5
  115.3 2.8 %collective-permute-start.4 = (bf16[4,2,128,128]{3,2,1,0:T(8,128)(2,1)}, bf16[4,2,128,128]{3,2,1,0:T(8,128)(2,1)S(1)}, u32[]{:S(2)}, u32[]{:S(2)}) collective-permute-start(bf16[4,2,128,128]{3,2,1,0:T(8,128)(2,1)} %get-tuple-element.6), channel_id=1, source_target_pairs={{0,2},{1,3},{2,0},{3,1},{4,6},{5,7},{6,4},{7,5},{8,10},{9,11},{10,... | collective-permute-start | bytes 786440 | tf_op jit(solution)/shard_map/ppermute | solution.py:177
  118.0 2.5 collective-permute-start.3
  121.2 0.2 fusion
  121.4 0.1 concatenate.3.info
  121.5 1.3 collective-permute-done.5.refs_3_
  122.8 3.2 %collective-permute-done.4.refs_2_ = bf16[4,2,128,128]{3,2,1,0:T(8,128)(2,1)S(1)} collective-permute-done((bf16[4,2,128,128]{3,2,1,0:T(8,128)(2,1)}, bf16[4,2,128,128]{3,2,1,0:T(8,128)(2,1)S(1)}, u32[]{:S(2)}, u32[]{:S(2)}) %collective-permute-start.4) | collective-permute-done | bytes 262176 | tf_op jit(solution)/shard_map/ppermute | solution.py:177
  126.0 0.7 copy-done.5
  126.7 6.0 %collective-permute-done.3.refs_1_ = bf16[4,2,128,128]{3,2,1,0:T(8,128)(2,1)S(1)} collective-permute-done((bf16[4,2,128,128]{3,2,1,0:T(8,128)(2,1)}, bf16[4,2,128,128]{3,2,1,0:T(8,128)(2,1)S(1)}, u32[]{:S(2)}, u32[]{:S(2)}) %collective-permute-start.3) | collective-permute-done | bytes 262176 | tf_op jit(solution)/shard_map/ppermute | solution.py:177
  132.7 0.7 copy-done.7
  133.4 0.9 copy-done.6
  134.4 0.9 copy-done.8
  135.3 10.4 %attend.1.refs_0_ = bf16[512,512]{1,0:T(8,128)(2,1)S(1)} custom-call(s32[21]{0:T(128)S(1)} %concatenate.3.info, bf16[512,512]{1,0:T(8,128)(2,1)} %bitcast.22.q_ref, bf16[4,2,128,128]{3,2,1,0:T(8,128)(2,1)S(1)} %get-tuple-element.8.refs_0_, bf16[4,2,128,128]{3,2,1,0:T(8,128)(2,1)S(1)} %copy-done.8, bf16[4,2,128,128]{3,2,1,0:T(8,128)(2,1)S(1)} %copy-done.6, ...), custom_call_target="tpu_custom_call" | custom-call | flops 2147483648 | bytes 2097152 | tf_op jit(solution)/shard_map/attend/pallas_call | solution.py:53
  145.7 1.9 collective-permute-start.8
  147.6 2.8 %collective-permute-start.7 = (bf16[512,512]{1,0:T(8,128)(2,1)S(1)}, bf16[512,512]{1,0:T(8,128)(2,1)}, u32[]{:S(2)}, u32[]{:S(2)}) collective-permute-start(bf16[512,512]{1,0:T(8,128)(2,1)S(1)} %attend.1.refs_0_), channel_id=1, source_target_pairs={{0,2},{1,3},{2,0},{3,1},{4,6},{5,7},{6,4},{7,5},{8,10},{9,11},{10,... | collective-permute-start | bytes 1572872 | tf_op jit(solution)/shard_map/ppermute | solution.py:193
  150.4 2.8 %collective-permute-start.6 = (bf16[512,512]{1,0:T(8,128)(2,1)S(1)}, bf16[512,512]{1,0:T(8,128)(2,1)}, u32[]{:S(2)}, u32[]{:S(2)}) collective-permute-start(bf16[512,512]{1,0:T(8,128)(2,1)S(1)} %attend.1.refs_0_), channel_id=1, source_target_pairs={{0,1},{1,2},{2,3},{3,0},{4,5},{5,6},{6,7},{7,4},{8,9},{9,10},{10,1... | collective-permute-start | bytes 1572872 | tf_op jit(solution)/shard_map/ppermute | solution.py:193
  153.2 0.1 stack.131.where
  153.3 7.4 %collective-permute-done.8.refs_3_ = bf16[512,512]{1,0:T(8,128)(2,1)} collective-permute-done((bf16[512,512]{1,0:T(8,128)(2,1)S(1)}, bf16[512,512]{1,0:T(8,128)(2,1)}, u32[]{:S(2)}, u32[]{:S(2)}) %collective-permute-start.8) | collective-permute-done | bytes 524320 | tf_op jit(solution)/shard_map/ppermute | solution.py:193
  160.7 2.9 %collective-permute-done.7.refs_2_ = bf16[512,512]{1,0:T(8,128)(2,1)} collective-permute-done((bf16[512,512]{1,0:T(8,128)(2,1)S(1)}, bf16[512,512]{1,0:T(8,128)(2,1)}, u32[]{:S(2)}, u32[]{:S(2)}) %collective-permute-start.7) | collective-permute-done | bytes 524320 | tf_op jit(solution)/shard_map/ppermute | solution.py:193
  163.6 12.6 %collective-permute-done.6.refs_1_ = bf16[512,512]{1,0:T(8,128)(2,1)} collective-permute-done((bf16[512,512]{1,0:T(8,128)(2,1)S(1)}, bf16[512,512]{1,0:T(8,128)(2,1)}, u32[]{:S(2)}, u32[]{:S(2)}) %collective-permute-start.6) | collective-permute-done | bytes 524320 | tf_op jit(solution)/shard_map/ppermute | solution.py:193
  176.2 4.4 %project.1 = bf16[4,512,256]{2,1,0:T(8,128)(2,1)S(1)} custom-call(s32[5]{0:T(128)S(1)} %stack.131.where, bf16[512,512]{1,0:T(8,128)(2,1)S(1)} %attend.1.refs_0_, bf16[512,512]{1,0:T(8,128)(2,1)} %collective-permute-done.6.refs_1_, bf16[512,512]{1,0:T(8,128)(2,1)} %collective-permute-done.7.refs_2_, bf16[512,512]{1,0:T(8,128)(2,1)} %collective-permute-done.8.refs_3_, ...), custom_call_target="tpu_custom_call" | custom-call | flops 2147483648 | bytes 8388608 | tf_op jit(solution)/shard_map/project/pallas_call | solution.py:120
  180.7 72.1 %all_to_all.10 = bf16[128,16,256]{2,1,0:T(8,128)(2,1)S(1)} all-to-all(bf16[128,16,256]{2,1,0:T(8,128)(2,1)S(1)} %bitcast.44), channel_id=1, replica_groups=mesh['zl'=4,'y'=4,'c'=2,'zh'=4,'x'=4] {'zh','zl','y','c'}, dimensions={0} | all-to-all | bytes 2097152 | tf_op jit(solution)/shard_map/all_to_all | solution.py:197
  252.8 0.1 bitcast_reduce_fusion
  252.9 0.8 add_convert_fusion
  (28 shorter events, 0.4 us)
Async XLA Ops:
  0.0 121.2 %copy-start = (s32[32,4]{0,1:T(4,128)S(1)}, s32[32,4]{0,1:T(4,128)}, u32[]{:S(2)}) copy-start(s32[32,4]{0,1:T(4,128)} %param.10) | copy-start | bytes 1540
  0.0 1.7 collective-permute-start.9
  1.7 32.5 %collective-permute-start.12 = (bf16[512,128]{1,0:T(8,128)(2,1)S(1)}, bf16[512,128]{1,0:T(8,128)(2,1)S(1)}, u32[]{:S(2)}, u32[]{:S(2)}) collective-permute-start(bf16[512,128]{1,0:T(8,128)(2,1)S(1)} %collective-permute-done.9), channel_id=1, source_target_pairs={{0,384},{128,0},{256,128},{384,256},{1,385},{129,1},{257,129},{385... | collective-permute-start | bytes 393224 | tf_op jit(solution)/shard_map/ppermute | solution.py:141
  3.6 30.6 %collective-permute-start.11 = (bf16[512,128]{1,0:T(8,128)(2,1)S(1)}, bf16[512,128]{1,0:T(8,128)(2,1)S(1)}, u32[]{:S(2)}, u32[]{:S(2)}) collective-permute-start(bf16[512,128]{1,0:T(8,128)(2,1)S(1)} %collective-permute-done.9), channel_id=1, source_target_pairs={{0,256},{128,384},{256,0},{384,128},{1,257},{129,385},{257,1},{385... | collective-permute-start | bytes 393224 | tf_op jit(solution)/shard_map/ppermute | solution.py:141
  8.5 25.7 %collective-permute-start.10 = (bf16[512,128]{1,0:T(8,128)(2,1)S(1)}, bf16[512,128]{1,0:T(8,128)(2,1)S(1)}, u32[]{:S(2)}, u32[]{:S(2)}) collective-permute-start(bf16[512,128]{1,0:T(8,128)(2,1)S(1)} %collective-permute-done.9), channel_id=1, source_target_pairs={{0,128},{128,256},{256,384},{384,0},{1,129},{129,257},{257,385},{3... | collective-permute-start | bytes 393224 | tf_op jit(solution)/shard_map/ppermute | solution.py:141
  14.8 118.6 %all-to-all-start = ((bf16[32,16,512]{2,1,0:T(8,128)(2,1)}), bf16[32,16,512]{2,1,0:T(8,128)(2,1)}, u32[]{:S(2)}, u32[]{:S(2)}) async-start(bf16[32,16,512]{2,1,0:T(8,128)(2,1)} %bitcast.21), calls=%async_computation | async-start | bytes 1048576 | tf_op jit(solution)/shard_map/all_to_all | solution.py:184
  34.3 19.0 %collective-permute-start.15 = (bf16[4,512,128]{2,1,0:T(8,128)(2,1)S(1)}, bf16[4,512,128]{2,1,0:T(8,128)(2,1)S(1)}, u32[]{:S(2)}, u32[]{:S(2)}) collective-permute-start(bf16[4,512,128]{2,1,0:T(8,128)(2,1)S(1)} %pad_maximum_fusion.1.refs_0_), channel_id=1, source_target_pairs={{0,96},{32,0},{64,32},{96,64},{1,97},{33,1},{65,33},{97,65},{2,98}... | collective-permute-start | bytes 1572872 | tf_op jit(solution)/shard_map/ppermute | solution.py:145
  38.6 18.5 %collective-permute-start.14 = (bf16[4,512,128]{2,1,0:T(8,128)(2,1)S(1)}, bf16[4,512,128]{2,1,0:T(8,128)(2,1)S(1)}, u32[]{:S(2)}, u32[]{:S(2)}) collective-permute-start(bf16[4,512,128]{2,1,0:T(8,128)(2,1)S(1)} %pad_maximum_fusion.1.refs_0_), channel_id=1, source_target_pairs={{0,64},{32,96},{64,0},{96,32},{1,65},{33,97},{65,1},{97,33},{2,66}... | collective-permute-start | bytes 1572872 | tf_op jit(solution)/shard_map/ppermute | solution.py:145
  41.1 27.8 %collective-permute-start.13 = (bf16[4,512,128]{2,1,0:T(8,128)(2,1)S(1)}, bf16[4,512,128]{2,1,0:T(8,128)(2,1)S(1)}, u32[]{:S(2)}, u32[]{:S(2)}) collective-permute-start(bf16[4,512,128]{2,1,0:T(8,128)(2,1)S(1)} %pad_maximum_fusion.1.refs_0_), channel_id=1, source_target_pairs={{0,32},{32,64},{64,96},{96,0},{1,33},{33,65},{65,97},{97,1},{2,34}... | collective-permute-start | bytes 1572872 | tf_op jit(solution)/shard_map/ppermute | solution.py:145
  57.1 0.8 copy-start.1
  68.9 0.8 copy-start.3
  69.7 1.0 copy-start.2
  70.7 1.0 copy-start.4
  71.7 3.2 %copy-start.10 = (bf16[1,128,1024]{2,1,0:T(8,128)(2,1)S(1)}, bf16[1,128,1024]{2,1,0:T(8,128)(2,1)}, u32[]{:S(2)}) copy-start(bf16[1,128,1024]{2,1,0:T(8,128)(2,1)} %param.11) | copy-start | bytes 786436
  72.7 103.6 %collective-permute-start.16 = (bf16[4,512,512]{2,1,0:T(8,128)(2,1)S(1)}, bf16[4,512,512]{2,1,0:T(8,128)(2,1)}, u32[]{:S(2)}, u32[]{:S(2)}) collective-permute-start(bf16[4,512,512]{2,1,0:T(8,128)(2,1)S(1)} %place.1.refs_4_), channel_id=1, source_target_pairs={{0,16},{16,0},{1,17},{17,1},{2,18},{18,2},{3,19},{19,3},{4,20},{20... | collective-permute-start | bytes 6291464 | tf_op jit(solution)/shard_map/ppermute | solution.py:148
  76.1 22.5 %collective-permute-start.2 = (bf16[2,128,256]{2,1,0:T(8,128)(2,1)S(1)}, bf16[2,128,256]{2,1,0:T(8,128)(2,1)S(1)}, u32[]{:S(2)}, u32[]{:S(2)}) collective-permute-start(bf16[2,128,256]{2,1,0:T(8,128)(2,1)S(1)} %get-tuple-element.10), channel_id=1, source_target_pairs={{0,12},{4,0},{8,4},{12,8},{1,13},{5,1},{9,5},{13,9},{2,14},{6,2},{... | collective-permute-start | bytes 393224 | tf_op jit(solution)/shard_map/ppermute | solution.py:169
  86.4 25.9 %collective-permute-start.1 = (bf16[2,128,256]{2,1,0:T(8,128)(2,1)S(1)}, bf16[2,128,256]{2,1,0:T(8,128)(2,1)S(1)}, u32[]{:S(2)}, u32[]{:S(2)}) collective-permute-start(bf16[2,128,256]{2,1,0:T(8,128)(2,1)S(1)} %get-tuple-element.11), channel_id=1, source_target_pairs={{0,8},{4,12},{8,0},{12,4},{1,9},{5,13},{9,1},{13,5},{2,10},{6,14},... | collective-permute-start | bytes 393224 | tf_op jit(solution)/shard_map/ppermute | solution.py:169
  91.9 20.4 %collective-permute-start = (bf16[2,128,256]{2,1,0:T(8,128)(2,1)S(1)}, bf16[2,128,256]{2,1,0:T(8,128)(2,1)S(1)}, u32[]{:S(2)}, u32[]{:S(2)}) collective-permute-start(bf16[2,128,256]{2,1,0:T(8,128)(2,1)S(1)} %get-tuple-element.12), channel_id=1, source_target_pairs={{0,4},{4,8},{8,12},{12,0},{1,5},{5,9},{9,13},{13,1},{2,6},{6,10},{... | collective-permute-start | bytes 393224 | tf_op jit(solution)/shard_map/ppermute | solution.py:169
  113.3 9.5 %collective-permute-start.5 = (bf16[4,2,128,128]{3,2,1,0:T(8,128)(2,1)}, bf16[4,2,128,128]{3,2,1,0:T(8,128)(2,1)S(1)}, u32[]{:S(2)}, u32[]{:S(2)}) collective-permute-start(bf16[4,2,128,128]{3,2,1,0:T(8,128)(2,1)} %get-tuple-element.5), channel_id=1, source_target_pairs={{0,3},{1,0},{2,1},{3,2},{4,7},{5,4},{6,5},{7,6},{8,11},{9,8},{10,9... | collective-permute-start | bytes 786440 | tf_op jit(solution)/shard_map/ppermute | solution.py:177
  115.3 10.7 %collective-permute-start.4 = (bf16[4,2,128,128]{3,2,1,0:T(8,128)(2,1)}, bf16[4,2,128,128]{3,2,1,0:T(8,128)(2,1)S(1)}, u32[]{:S(2)}, u32[]{:S(2)}) collective-permute-start(bf16[4,2,128,128]{3,2,1,0:T(8,128)(2,1)} %get-tuple-element.6), channel_id=1, source_target_pairs={{0,2},{1,3},{2,0},{3,1},{4,6},{5,7},{6,4},{7,5},{8,10},{9,11},{10,... | collective-permute-start | bytes 786440 | tf_op jit(solution)/shard_map/ppermute | solution.py:177
  118.0 14.7 %collective-permute-start.3 = (bf16[4,2,128,128]{3,2,1,0:T(8,128)(2,1)}, bf16[4,2,128,128]{3,2,1,0:T(8,128)(2,1)S(1)}, u32[]{:S(2)}, u32[]{:S(2)}) collective-permute-start(bf16[4,2,128,128]{3,2,1,0:T(8,128)(2,1)} %get-tuple-element.7), channel_id=1, source_target_pairs={{0,1},{1,2},{2,3},{3,0},{4,5},{5,6},{6,7},{7,4},{8,9},{9,10},{10,1... | collective-permute-start | bytes 786440 | tf_op jit(solution)/shard_map/ppermute | solution.py:177
  126.0 0.7 copy-start.5
  132.7 0.7 copy-start.7
  133.4 1.0 copy-start.6
  134.4 0.9 copy-start.8
  145.7 15.0 %collective-permute-start.8 = (bf16[512,512]{1,0:T(8,128)(2,1)S(1)}, bf16[512,512]{1,0:T(8,128)(2,1)}, u32[]{:S(2)}, u32[]{:S(2)}) collective-permute-start(bf16[512,512]{1,0:T(8,128)(2,1)S(1)} %attend.1.refs_0_), channel_id=1, source_target_pairs={{0,3},{1,0},{2,1},{3,2},{4,7},{5,4},{6,5},{7,6},{8,11},{9,8},{10,9... | collective-permute-start | bytes 1572872 | tf_op jit(solution)/shard_map/ppermute | solution.py:193
  147.6 16.0 %collective-permute-start.7 = (bf16[512,512]{1,0:T(8,128)(2,1)S(1)}, bf16[512,512]{1,0:T(8,128)(2,1)}, u32[]{:S(2)}, u32[]{:S(2)}) collective-permute-start(bf16[512,512]{1,0:T(8,128)(2,1)S(1)} %attend.1.refs_0_), channel_id=1, source_target_pairs={{0,2},{1,3},{2,0},{3,1},{4,6},{5,7},{6,4},{7,5},{8,10},{9,11},{10,... | collective-permute-start | bytes 1572872 | tf_op jit(solution)/shard_map/ppermute | solution.py:193
  150.4 25.8 %collective-permute-start.6 = (bf16[512,512]{1,0:T(8,128)(2,1)S(1)}, bf16[512,512]{1,0:T(8,128)(2,1)}, u32[]{:S(2)}, u32[]{:S(2)}) collective-permute-start(bf16[512,512]{1,0:T(8,128)(2,1)S(1)} %attend.1.refs_0_), channel_id=1, source_target_pairs={{0,1},{1,2},{2,3},{3,0},{4,5},{5,6},{6,7},{7,4},{8,9},{9,10},{10,1... | collective-permute-start | bytes 1572872 | tf_op jit(solution)/shard_map/ppermute | solution.py:193
  180.7 72.3 %copy-start.9 = (bf16[512,256]{1,0:T(8,128)(2,1)S(1)}, bf16[512,256]{1,0:T(8,128)(2,1)}, u32[]{:S(2)}) copy-start(bf16[512,256]{1,0:T(8,128)(2,1)} %param.15) | copy-start | bytes 786436
where the time goes:
time: 255 us; the launch traced here: 254 us
  starting transfers between devices  80.8 us (32%)
  blocking collectives  72.1 us (28%)
  waiting for transfers between devices  71.5 us (28%)
  Pallas kernels  15.7 us (6%)
  local copies, waits for them, and re-layouts  9.53 us (4%)
  other arithmetic  3.08 us (1%)
    all_to_all x1, blocking collectives, step(): returned = lax.all_to_all(partial, ('zh',) + VAR, 0, 0, tiled=True)  72.1 us
    ppermute x3, waiting for transfers between devices, gather_weight(): parts.append(lax.ppermute(along, 'y', shifted(4, s)))  24.4 us
    ppermute x3, waiting for transfers between devices, step(): gathered.append(lax.ppermute(gated, 'x', shifted(4, s)))  22.9 us
    ppermute x3, starting transfers between devices, step(): kv.append(lax.ppermute(heads_for(zh + s & 3), 'zh', shifted(4, s)))  22.5 us
    all_to_all x1, starting transfers between devices, step(): lax.all_to_all(marked.reshape(prompts, per_prompt, feature_count), VAR, 0...  19.3 us
    ppermute x3, waiting for transfers between devices, step(): kv.append(lax.ppermute(heads_for(zh + s & 3), 'zh', shifted(4, s)))  13.7 us
    ppermute x3, starting transfers between devices, gather_weight(): along.append(lax.ppermute(turned, 'zl', shifted(4, s)))  11.1 us
    ppermute x3, waiting for transfers between devices, step(): kv_here.append(lax.ppermute(head_for(x + t & 3), 'x', shifted(4, t)))  10.5 us
  transfers between devices with their start and end apart: 18, of which 10 were waited for; matrix products, arithmetic and copies ran while one was open for 2% of the time, Pallas kernels for 4%

commit v1 on v0

--- a/solution.py
+++ b/solution.py
@@ -11,39 +11,49 @@
 HD = 128
 VAR = ("zl", "y", "c")
 HEAD = ("zh", "x")
-ROW_BLOCK = 128
+ROW_BLOCK = 256
+DEAD = -1e30
 
 
 def attend_kernel(info, q_ref, *refs):
     kv, (out_ref, k_all, v_all) = refs[:-3], refs[-3:]
     slots, _, span, _ = kv[0].shape
-    base = 1 + q_ref.shape[1] // HD
+    rows, feats = q_ref.shape
+    heads = feats // HD
+    base = 1 + heads
 
     @pl.when(pl.program_id(0) == 0)
     def _():
         for t, kv_ref in enumerate(kv):
             for s in range(slots):
-                at = pl.ds(pl.multiple_of(info[base + t * slots + s] * span, span), span)
-                k_all[at, :] = kv_ref[s, 0]
-                v_all[at, :] = kv_ref[s, 1]
-
-    positions = k_all.shape[0]
-    live = lax.broadcasted_iota(jnp.int32, (1, positions), 1) < info[0]
-    bias = jnp.where(live, 0.0, -jnp.inf).astype(jnp.float32)
+                first = pl.multiple_of(info[base + t * slots + s] * span, span)
+                at = pl.ds(first, span)
+                position = first + lax.broadcasted_iota(jnp.int32, (span, HD), 0)
+                k_all[at, :HD] = kv_ref[s, 0]
+                k_all[at, HD:] = jnp.where(position < info[0], 0.0, DEAD).astype(jnp.bfloat16)
+                v_all[at, :HD] = kv_ref[s, 1]
+                v_all[at, HD:] = jnp.ones((span, HD), jnp.bfloat16)
+
     scale = math.log2(math.e) / math.sqrt(HD)
-    for j in range(q_ref.shape[1] // HD):
-        cols = slice(j * HD, (j + 1) * HD)
-        scores = lax.dot_general(
-            q_ref[:, cols], k_all[...], (((1,), (1,)), ((), ())), preferred_element_type=jnp.float32
+    one = (lax.broadcasted_iota(jnp.int32, (rows, HD), 1) == 0).astype(jnp.bfloat16)
+
+    def scores_of(j):
+        query = jnp.concatenate([q_ref[:, j * HD : (j + 1) * HD], one], axis=1)
+        return lax.dot_general(
+            query, k_all[...], (((1,), (1,)), ((), ())), preferred_element_type=jnp.float32
         )
-        scores = scores * scale + bias
+
+    scores = scores_of(0)
+    for j in range(heads):
+        following = scores_of(j + 1) if j + 1 < heads else None
         top = jnp.max(scores, axis=-1, keepdims=True)
-        weight = jnp.exp2(scores - top)
-        total = jnp.sum(weight, axis=-1, keepdims=True)
-        mixed = jnp.dot(weight.astype(jnp.bfloat16), v_all[...], preferred_element_type=jnp.float32)
-        first = q_ref[:, j * HD : j * HD + 1].astype(jnp.float32)
-        keep = jnp.logical_and(first != jnp.inf, info[1 + j] != 0)
-        out_ref[:, cols] = jnp.where(keep, mixed / total, 0.0).astype(jnp.bfloat16)
+        weight = jnp.exp2((scores - top) * scale).astype(jnp.bfloat16)
+        mixed = jnp.dot(weight, v_all[...], preferred_element_type=jnp.float32)
+        mixed = mixed[:, :HD] / mixed[:, HD : HD + 1]
+        mark = q_ref[:, j * HD : j * HD + 1].astype(jnp.float32)
+        keep = jnp.logical_and(mark != jnp.inf, info[1 + j] != 0)
+        out_ref[:, j * HD : (j + 1) * HD] = jnp.where(keep, mixed, 0.0).astype(jnp.bfloat16)
+        scores = following
 
 
 def attend(info, queries, kv):
@@ -60,8 +70,8 @@
             + [pl.BlockSpec(kv[0].shape, lambda i, s: (0, 0, 0, 0))] * len(kv),
             out_specs=pl.BlockSpec((ROW_BLOCK, feats), lambda i, s: (i, 0)),
             scratch_shapes=[
-                pltpu.VMEM((positions, HD), jnp.bfloat16),
-                pltpu.VMEM((positions, HD), jnp.bfloat16),
+                pltpu.VMEM((positions, 2 * HD), jnp.bfloat16),
+                pltpu.VMEM((positions, 2 * HD), jnp.bfloat16),
             ],
         ),
         cost_estimate=pl.CostEstimate(
@@ -69,46 +79,52 @@
             transcendentals=rows * (feats // HD) * positions,
             bytes_accessed=4 * rows * feats + 4 * positions * HD,
         ),
-        compiler_params=pltpu.CompilerParams(vmem_limit_bytes=40 << 20),
+        compiler_params=pltpu.CompilerParams(vmem_limit_bytes=24 << 20),
         name="attend",
     )(info, queries, *kv)
 
 
 def place_kernel(where, *refs):
-    parts, out_ref = refs[:-1], refs[-1]
-    for t, part in enumerate(parts):
+    parts, (out_ref, held, sems) = refs[:-3], refs[-3:]
+    copies = [pltpu.make_async_copy(part, held.at[t], sems.at[t]) for t, part in enumerate(parts)]
+    for copy in copies:
+        copy.start()
+    for t, copy in enumerate(copies):
+        copy.wait()
         for s in range(4):
-            out_ref[where[t], :, pl.ds(pl.multiple_of(where[4 + s] * 128, 128), 128)] = part[s]
+            out_ref[where[t], :, pl.ds(pl.multiple_of(where[4 + s] * 128, 128), 128)] = held[t, s]
 
 
 def place(where, parts):
-    spec = pl.BlockSpec(memory_space=pltpu.VMEM)
     return pl.pallas_call(
         place_kernel,
         out_shape=jax.ShapeDtypeStruct((4, 512, 512), jnp.bfloat16),
-        in_specs=[pl.BlockSpec(memory_space=pltpu.SMEM)] + [spec] * len(parts),
-        out_specs=spec,
+        in_specs=[pl.BlockSpec(memory_space=pltpu.SMEM)] + [pl.BlockSpec(memory_space=pl.ANY)] * len(parts),
+        out_specs=pl.BlockSpec(memory_space=pltpu.VMEM),
+        scratch_shapes=[
+            pltpu.VMEM((len(parts), 4, 512, 128), jnp.bfloat16),
+            pltpu.SemaphoreType.DMA((len(parts),)),
+        ],
         cost_estimate=pl.CostEstimate(flops=0, transcendentals=0, bytes_accessed=4 << 20),
-        compiler_params=pltpu.CompilerParams(vmem_limit_bytes=16 << 20),
         name="place",
     )(where, *parts)
 
 
 def project_kernel(where, *refs):
-    gated, (own_ref, other_ref, out_ref) = refs[:-3], refs[-3:]
+    gated, (own_ref, other_any, out_ref, other_ref, sem) = refs[:-5], refs[-5:]
+    fetch = pltpu.make_async_copy(other_any, other_ref, sem)
+    fetch.start()
     c = where[0]
+    rows = jnp.concatenate([g_ref[...] for g_ref in gated], axis=1)
     for u, w_ref in enumerate((own_ref, other_ref)):
+        if u == 1:
+            fetch.wait()
         lanes = pl.ds(pl.multiple_of((c if u == 0 else 1 - c) * 128, 128), 128)
         for pair in range(2):
-            total = None
-            for s, g_ref in enumerate(gated):
-                term = jnp.dot(
-                    g_ref[...],
-                    w_ref[where[1 + s], :, pair * 256 : (pair + 1) * 256],
-                    preferred_element_type=jnp.float32,
-                )
-                total = term if total is None else total + term
-            total = total.astype(jnp.bfloat16)
+            weight = [w_ref[where[1 + s], :, pair * 256 : (pair + 1) * 256] for s in range(len(gated))]
+            total = jnp.dot(
+                rows, jnp.concatenate(weight, axis=0), preferred_element_type=jnp.float32
+            ).astype(jnp.bfloat16)
             out_ref[2 * pair, :, lanes] = total[:, :128]
             out_ref[2 * pair + 1, :, lanes] = total[:, 128:]
 
@@ -120,12 +136,15 @@
     return pl.pallas_call(
         project_kernel,
         out_shape=jax.ShapeDtypeStruct((4, rows, 256), jnp.bfloat16),
-        in_specs=[pl.BlockSpec(memory_space=pltpu.SMEM)] + [spec] * (parts + 2),
+        in_specs=[pl.BlockSpec(memory_space=pltpu.SMEM)]
+        + [spec] * (parts + 1)
+        + [pl.BlockSpec(memory_space=pl.ANY)],
         out_specs=spec,
+        scratch_shapes=[pltpu.VMEM(other.shape, other.dtype), pltpu.SemaphoreType.DMA],
         cost_estimate=pl.CostEstimate(
             flops=2 * parts * rows * feats * 1024, transcendentals=0, bytes_accessed=8 << 20
         ),
-        compiler_params=pltpu.CompilerParams(vmem_limit_bytes=24 << 20),
+        compiler_params=pltpu.CompilerParams(vmem_limit_bytes=16 << 20),
         name="project",
     )(where, *gated, own, other)
 
@@ -136,14 +155,13 @@
 
 def gather_weight(out_weight, y, zl):
     turned = lax.ppermute(out_weight, ("y", "x"), [(y * 4 + x, x * 4 + y) for y in range(4) for x in range(4)])
-    along = [turned]
-    for s in (1, 2, 3):
-        along.append(lax.ppermute(turned, "zl", shifted(4, s)))
-    along = jnp.stack(along)
+    pair = jnp.stack([turned, lax.ppermute(turned, "zl", [(i, i ^ 1) for i in range(4)])])
+    far = lax.ppermute(pair, "zl", [(i, i ^ 2) for i in range(4)])
+    along = jnp.concatenate([pair, far])
     parts = [along]
     for s in (1, 2, 3):
         parts.append(lax.ppermute(along, "y", shifted(4, s)))
-    where = jnp.stack([(y + 4 - t) & 3 for t in range(4)] + [(zl + 4 - s) & 3 for s in range(4)])
+    where = jnp.stack([(y + 4 - t) & 3 for t in range(4)] + [zl ^ s for s in range(4)])
     own = place(where.astype(jnp.int32), parts)
     other = lax.ppermute(own, "c", [(0, 1), (1, 0)])
     return own, other
@@ -159,10 +177,10 @@
     first_head = head_position * local_heads
 
     zh = lax.axis_index("zh")
-    caches = jnp.stack([k_cache[0], v_cache[0]])
 
     def heads_for(other_zh):
-        return lax.dynamic_slice_in_dim(caches, other_zh * (2 * HD), 2 * HD, 2)
+        first = other_zh * (2 * HD)
+        return jnp.stack([lax.dynamic_slice_in_dim(c[0], first, 2 * HD, 1) for c in (k_cache, v_cache)])
 
     kv = [heads_for(zh)]
     for s in (1, 2, 3):

time: 255 us -> 248 us (0.973)
  starting transfers between devices: 80.8 us -> 77.8 us
    ppermute x3 -> x2, waiting for transfers between devices: 0.01 us -> 3.78 us  [the longest x1 3.77 us: gather_weight(): lax.ppermute(turned, 'zl', [(i, i ^ 1) for i in range(4)])]
    ppermute x3 -> x2, starting transfers between devices: 11.1 us -> 7.37 us  [the longest x1 5.46 us: gather_weight(): far = lax.ppermute(pair, 'zl', [(i, i ^ 2) for i in range(4)])]
    pallas_call x1, Pallas kernels: 10.4 us -> 6.99 us  [attend(): pl.pallas_call(attend_kernel, out_shape=jax.ShapeDtypeStruct((rows, feats...]
    ppermute x3, starting transfers between devices: 9.27 us -> 12.1 us  [gather_weight(): parts.append(lax.ppermute(along, 'y', shifted(4, s)))]
    pallas_call x1, Pallas kernels: 0.9 us -> 3.64 us  [place(): pl.pallas_call(place_kernel, out_shape=jax.ShapeDtypeStruct((4, 512, 512)...]
    unnamed x23 -> x30, local copies, waits for them, and re-layouts: 7.03 us -> 5.78 us
  transfers between devices with their start and end apart: 18 -> 17, of which waited for: 10 -> 9; matrix products, arithmetic and copies ran while one was open for 2% -> 1% of each run, Pallas kernels for 4% -> 4%
where the time goes in v1:
time: 248 us; the launch traced here: 247 us
  starting transfers between devices  77.8 us (31%)
  waiting for transfers between devices  72.5 us (29%)
  blocking collectives  69.7 us (28%)
  Pallas kernels  15.8 us (6%)
  local copies, waits for them, and re-layouts  7.08 us (3%)
  other arithmetic  3.17 us (1%)
    all_to_all x1, blocking collectives, step(): returned = lax.all_to_all(partial, ('zh',) + VAR, 0, 0, tiled=True)  69.7 us
    ppermute x3, waiting for transfers between devices, gather_weight(): parts.append(lax.ppermute(along, 'y', shifted(4, s)))  24.1 us
    ppermute x3, waiting for transfers between devices, step(): gathered.append(lax.ppermute(gated, 'x', shifted(4, s)))  23.2 us
    ppermute x3, starting transfers between devices, step(): kv.append(lax.ppermute(heads_for(zh + s & 3), 'zh', shifted(4, s)))  20.9 us
    all_to_all x1, starting transfers between devices, step(): lax.all_to_all(marked.reshape(prompts, per_prompt, feature_count), VAR, 0...  19 us
    ppermute x3, waiting for transfers between devices, step(): kv.append(lax.ppermute(heads_for(zh + s & 3), 'zh', shifted(4, s)))  12.6 us
    ppermute x3, starting transfers between devices, gather_weight(): parts.append(lax.ppermute(along, 'y', shifted(4, s)))  12.1 us
    ppermute x3, waiting for transfers between devices, step(): kv_here.append(lax.ppermute(head_for(x + t & 3), 'x', shifted(4, t)))  8.85 us
  transfers between devices with their start and end apart: 17, of which 9 were waited for; matrix products, arithmetic and copies ran while one was open for 1% of the time, Pallas kernels for 4%

profile of v1, /device:TPU:33, one launch (start us, length us, event | category | flops | bytes accessed | tf_op | source)
XLA Modules:
  0.0 247.2 jit_solution(8378506724000341238)
XLA Ops:
  0.0 1.7 collective-permute-start.9
  1.7 1.9 collective-permute-start.10
  3.6 3.8 %collective-permute-done.10 = bf16[512,128]{1,0:T(8,128)(2,1)S(1)} collective-permute-done((bf16[512,128]{1,0:T(8,128)(2,1)S(1)}, bf16[512,128]{1,0:T(8,128)(2,1)S(1)}, u32[]{:S(2)}, u32[]{:S(2)}) %collective-permute-start.10) | collective-permute-done | bytes 131104 | tf_op jit(solution)/shard_map/ppermute | solution.py:158
  7.4 5.5 %collective-permute-start.11 = (bf16[2,512,128]{2,1,0:T(8,128)(2,1)S(1)}, bf16[2,512,128]{2,1,0:T(8,128)(2,1)S(1)}, u32[]{:S(2)}, u32[]{:S(2)}) collective-permute-start(bf16[2,512,128]{2,1,0:T(8,128)(2,1)S(1)} %pad_maximum_fusion.2), channel_id=1, source_target_pairs={{0,256},{128,384},{256,0},{384,128},{1,257},{129,385},{257,1},{385... | collective-permute-start | bytes 786440 | tf_op jit(solution)/shard_map/ppermute | solution.py:159
  12.9 2.0 compare_select_fusion
  15.0 19.0 %all-to-all-start = ((bf16[32,16,512]{2,1,0:T(8,128)(2,1)}), bf16[32,16,512]{2,1,0:T(8,128)(2,1)S(1)}, u32[]{:S(2)}, u32[]{:S(2)}) async-start(bf16[32,16,512]{2,1,0:T(8,128)(2,1)} %bitcast.21), calls=%async_computation | async-start | bytes 1048576 | tf_op jit(solution)/shard_map/all_to_all | solution.py:202
  33.9 0.1 pad_maximum_fusion.1.refs_0_
  34.0 7.7 %collective-permute-start.14 = (bf16[4,512,128]{2,1,0:T(8,128)(2,1)S(1)}, bf16[4,512,128]{2,1,0:T(8,128)(2,1)S(1)}, u32[]{:S(2)}, u32[]{:S(2)}) collective-permute-start(bf16[4,512,128]{2,1,0:T(8,128)(2,1)S(1)} %pad_maximum_fusion.1.refs_0_), channel_id=1, source_target_pairs={{0,96},{32,0},{64,32},{96,64},{1,97},{33,1},{65,33},{97,65},{2,98}... | collective-permute-start | bytes 1572872 | tf_op jit(solution)/shard_map/ppermute | solution.py:163
  41.7 1.9 collective-permute-start.13
  43.6 2.5 %collective-permute-start.12 = (bf16[4,512,128]{2,1,0:T(8,128)(2,1)S(1)}, bf16[4,512,128]{2,1,0:T(8,128)(2,1)S(1)}, u32[]{:S(2)}, u32[]{:S(2)}) collective-permute-start(bf16[4,512,128]{2,1,0:T(8,128)(2,1)S(1)} %pad_maximum_fusion.1.refs_0_), channel_id=1, source_target_pairs={{0,32},{32,64},{64,96},{96,0},{1,33},{33,65},{65,97},{97,1},{2,34}... | collective-permute-start | bytes 1572872 | tf_op jit(solution)/shard_map/ppermute | solution.py:163
  46.1 0.7 stack.176.where
  46.8 17.3 %collective-permute-done.14.refs_3_ = bf16[4,512,128]{2,1,0:T(8,128)(2,1)S(1)} collective-permute-done((bf16[4,512,128]{2,1,0:T(8,128)(2,1)S(1)}, bf16[4,512,128]{2,1,0:T(8,128)(2,1)S(1)}, u32[]{:S(2)}, u32[]{:S(2)}) %collective-permute-start.14) | collective-permute-done | bytes 524320 | tf_op jit(solution)/shard_map/ppermute | solution.py:163
  64.1 6.8 %collective-permute-done.12.refs_1_ = bf16[4,512,128]{2,1,0:T(8,128)(2,1)S(1)} collective-permute-done((bf16[4,512,128]{2,1,0:T(8,128)(2,1)S(1)}, bf16[4,512,128]{2,1,0:T(8,128)(2,1)S(1)}, u32[]{:S(2)}, u32[]{:S(2)}) %collective-permute-start.12) | collective-permute-done | bytes 524320 | tf_op jit(solution)/shard_map/ppermute | solution.py:163
  70.9 0.8 copy-done.11
  71.7 3.6 %place.1.refs_4_ = bf16[4,512,512]{2,1,0:T(8,128)(2,1)} custom-call(s32[8]{0:T(128)} %stack.176.where, bf16[4,512,128]{2,1,0:T(8,128)(2,1)} %copy-done.8, bf16[4,512,128]{2,1,0:T(8,128)(2,1)} %copy-done.11, bf16[4,512,128]{2,1,0:T(8,128)(2,1)} %copy-done.10, bf16[4,512,128]{2,1,0:T(8,128)(2,1)} %copy-done.9), custom_call_target="tpu_custom_call" | custom-call | bytes 4194304 | tf_op jit(solution)/shard_map/place/pallas_call | solution.py:99
  75.3 2.3 collective-permute-start.15
  77.7 0.1 constant_dynamic-slice_fusion.10
  77.8 11.7 %collective-permute-start.1 = (bf16[2,128,256]{2,1,0:T(8,128)(2,1)S(1)}, bf16[2,128,256]{2,1,0:T(8,128)(2,1)S(1)}, u32[]{:S(2)}, u32[]{:S(2)}) collective-permute-start(bf16[2,128,256]{2,1,0:T(8,128)(2,1)S(1)} %pad_maximum_fusion.4), channel_id=1, source_target_pairs={{0,8},{4,12},{8,0},{12,4},{1,9},{5,13},{9,1},{13,5},{2,10},{6,14},... | collective-permute-start | bytes 393224 | tf_op jit(solution)/shard_map/ppermute | solution.py:187
  89.6 4.1 %collective-permute-start.2 = (bf16[2,128,256]{2,1,0:T(8,128)(2,1)S(1)}, bf16[2,128,256]{2,1,0:T(8,128)(2,1)S(1)}, u32[]{:S(2)}, u32[]{:S(2)}) collective-permute-start(bf16[2,128,256]{2,1,0:T(8,128)(2,1)S(1)} %pad_maximum_fusion.5), channel_id=1, source_target_pairs={{0,12},{4,0},{8,4},{12,8},{1,13},{5,1},{9,5},{13,9},{2,14},{6,2},{... | collective-permute-start | bytes 393224 | tf_op jit(solution)/shard_map/ppermute | solution.py:187
  93.7 5.1 %collective-permute-start = (bf16[2,128,256]{2,1,0:T(8,128)(2,1)S(1)}, bf16[2,128,256]{2,1,0:T(8,128)(2,1)S(1)}, u32[]{:S(2)}, u32[]{:S(2)}) collective-permute-start(bf16[2,128,256]{2,1,0:T(8,128)(2,1)S(1)} %pad_maximum_fusion.3), channel_id=1, source_target_pairs={{0,4},{4,8},{8,12},{12,0},{1,5},{5,9},{9,13},{13,1},{2,6},{6,10},{... | collective-permute-start | bytes 393224 | tf_op jit(solution)/shard_map/ppermute | solution.py:187
  98.8 12.6 %collective-permute-done.2 = bf16[2,128,256]{2,1,0:T(8,128)(2,1)S(1)} collective-permute-done((bf16[2,128,256]{2,1,0:T(8,128)(2,1)S(1)}, bf16[2,128,256]{2,1,0:T(8,128)(2,1)S(1)}, u32[]{:S(2)}, u32[]{:S(2)}) %collective-permute-start.2) | collective-permute-done | bytes 131104 | tf_op jit(solution)/shard_map/ppermute | solution.py:187
  111.5 0.1 pad_maximum_fusion
  111.5 0.2 constant_dynamic-slice_fusion
  111.8 2.0 collective-permute-start.5
  113.7 1.9 collective-permute-start.4
  115.6 3.3 %collective-permute-start.3 = (bf16[4,2,128,128]{3,2,1,0:T(8,128)(2,1)S(1)}, bf16[4,2,128,128]{3,2,1,0:T(8,128)(2,1)S(1)}, u32[]{:S(2)}, u32[]{:S(2)}) collective-permute-start(bf16[4,2,128,128]{3,2,1,0:T(8,128)(2,1)S(1)} %get-tuple-element.7), channel_id=1, source_target_pairs={{0,1},{1,2},{2,3},{3,0},{4,5},{5,6},{6,7},{7,4},{8,9},{9,10},{10,1... | collective-permute-start | bytes 786440 | tf_op jit(solution)/shard_map/ppermute | solution.py:195
  119.7 0.2 fusion.1
  119.9 0.1 concatenate.7.info
  120.0 0.7 copy-done.2
  120.7 2.2 collective-permute-done.4.refs_2_
  122.9 0.7 copy-done.4
  123.6 6.6 %collective-permute-done.3.refs_1_ = bf16[4,2,128,128]{3,2,1,0:T(8,128)(2,1)S(1)} collective-permute-done((bf16[4,2,128,128]{3,2,1,0:T(8,128)(2,1)S(1)}, bf16[4,2,128,128]{3,2,1,0:T(8,128)(2,1)S(1)}, u32[]{:S(2)}, u32[]{:S(2)}) %collective-permute-start.3) | collective-permute-done | bytes 262176 | tf_op jit(solution)/shard_map/ppermute | solution.py:195
  130.2 0.7 copy-done.6
  130.9 0.9 copy-done.3
  131.9 0.9 copy-done.5
  132.8 0.9 copy-done.7
  133.8 7.0 %attend.1.refs_0_ = bf16[512,512]{1,0:T(8,128)(2,1)S(1)} custom-call(s32[21]{0:T(128)S(1)} %concatenate.7.info, bf16[512,512]{1,0:T(8,128)(2,1)S(1)} %bitcast.43, bf16[4,2,128,128]{3,2,1,0:T(8,128)(2,1)S(1)} %get-tuple-element.8.refs_0_, bf16[4,2,128,128]{3,2,1,0:T(8,128)(2,1)S(1)} %copy-done.7, bf16[4,2,128,128]{3,2,1,0:T(8,128)(2,1)S(1)} %copy-done.5, ...), custom_call_target="tpu_custom_call" | custom-call | flops 2147483648 | bytes 2097152 | tf_op jit(solution)/shard_map/attend/pallas_call | solution.py:63
  140.8 1.9 collective-permute-start.8
  142.7 1.9 collective-permute-start.7
  144.7 3.4 %collective-permute-start.6 = (bf16[512,512]{1,0:T(8,128)(2,1)S(1)}, bf16[512,512]{1,0:T(8,128)(2,1)}, u32[]{:S(2)}, u32[]{:S(2)}) collective-permute-start(bf16[512,512]{1,0:T(8,128)(2,1)S(1)} %attend.1.refs_0_), channel_id=1, source_target_pairs={{0,1},{1,2},{2,3},{3,0},{4,5},{5,6},{6,7},{7,4},{8,9},{9,10},{10,1... | collective-permute-start | bytes 1572872 | tf_op jit(solution)/shard_map/ppermute | solution.py:211
  148.0 0.1 stack.142.where
  148.1 6.9 %collective-permute-done.8.refs_3_ = bf16[512,512]{1,0:T(8,128)(2,1)S(1)} collective-permute-done((bf16[512,512]{1,0:T(8,128)(2,1)S(1)}, bf16[512,512]{1,0:T(8,128)(2,1)S(1)}, u32[]{:S(2)}, u32[]{:S(2)}) %collective-permute-start.8) | collective-permute-done | bytes 524320 | tf_op jit(solution)/shard_map/ppermute | solution.py:211
  155.0 2.9 %collective-permute-done.7.refs_2_ = bf16[512,512]{1,0:T(8,128)(2,1)} collective-permute-done((bf16[512,512]{1,0:T(8,128)(2,1)S(1)}, bf16[512,512]{1,0:T(8,128)(2,1)}, u32[]{:S(2)}, u32[]{:S(2)}) %collective-permute-start.7) | collective-permute-done | bytes 524320 | tf_op jit(solution)/shard_map/ppermute | solution.py:211
  158.0 13.3 %collective-permute-done.6.refs_1_ = bf16[512,512]{1,0:T(8,128)(2,1)} collective-permute-done((bf16[512,512]{1,0:T(8,128)(2,1)S(1)}, bf16[512,512]{1,0:T(8,128)(2,1)}, u32[]{:S(2)}, u32[]{:S(2)}) %collective-permute-start.6) | collective-permute-done | bytes 524320 | tf_op jit(solution)/shard_map/ppermute | solution.py:211
  171.3 5.2 %project.1 = bf16[4,512,256]{2,1,0:T(8,128)(2,1)S(1)} custom-call(s32[5]{0:T(128)S(1)} %stack.142.where, bf16[512,512]{1,0:T(8,128)(2,1)S(1)} %attend.1.refs_0_, bf16[512,512]{1,0:T(8,128)(2,1)} %collective-permute-done.6.refs_1_, bf16[512,512]{1,0:T(8,128)(2,1)} %collective-permute-done.7.refs_2_, bf16[512,512]{1,0:T(8,128)(2,1)S(1)} %collective-permute-done.8.refs_3_, ...), custom_call_target="tpu_custom_call" | custom-call | flops 2147483648 | bytes 8388608 | tf_op jit(solution)/shard_map/project/pallas_call | solution.py:136
  176.5 69.7 %all_to_all.10 = bf16[128,16,256]{2,1,0:T(8,128)(2,1)S(1)} all-to-all(bf16[128,16,256]{2,1,0:T(8,128)(2,1)S(1)} %bitcast.42), channel_id=1, replica_groups=mesh['zl'=4,'y'=4,'c'=2,'zh'=4,'x'=4] {'zh','zl','y','c'}, dimensions={0} | all-to-all | bytes 2097152 | tf_op jit(solution)/shard_map/all_to_all | solution.py:215
  246.3 0.1 bitcast_reduce_fusion
  246.4 0.8 add_convert_fusion
  (37 shorter events, 0.2 us)
Async XLA Ops:
  0.0 119.7 %copy-start = (s32[32,4]{0,1:T(4,128)S(1)}, s32[32,4]{0,1:T(4,128)}, u32[]{:S(2)}) copy-start(s32[32,4]{0,1:T(4,128)} %param.10) | copy-start | bytes 1540
  0.0 1.7 collective-permute-start.9
  1.7 5.7 %collective-permute-start.10 = (bf16[512,128]{1,0:T(8,128)(2,1)S(1)}, bf16[512,128]{1,0:T(8,128)(2,1)S(1)}, u32[]{:S(2)}, u32[]{:S(2)}) collective-permute-start(bf16[512,128]{1,0:T(8,128)(2,1)S(1)} %collective-permute-done.9), channel_id=1, source_target_pairs={{0,128},{128,0},{256,384},{384,256},{1,129},{129,1},{257,385},{385... | collective-permute-start | bytes 393224 | tf_op jit(solution)/shard_map/ppermute | solution.py:158
  7.4 26.5 %collective-permute-start.11 = (bf16[2,512,128]{2,1,0:T(8,128)(2,1)S(1)}, bf16[2,512,128]{2,1,0:T(8,128)(2,1)S(1)}, u32[]{:S(2)}, u32[]{:S(2)}) collective-permute-start(bf16[2,512,128]{2,1,0:T(8,128)(2,1)S(1)} %pad_maximum_fusion.2), channel_id=1, source_target_pairs={{0,256},{128,384},{256,0},{384,128},{1,257},{129,385},{257,1},{385... | collective-permute-start | bytes 786440 | tf_op jit(solution)/shard_map/ppermute | solution.py:159
  15.0 116.0 %all-to-all-start = ((bf16[32,16,512]{2,1,0:T(8,128)(2,1)}), bf16[32,16,512]{2,1,0:T(8,128)(2,1)S(1)}, u32[]{:S(2)}, u32[]{:S(2)}) async-start(bf16[32,16,512]{2,1,0:T(8,128)(2,1)} %bitcast.21), calls=%async_computation | async-start | bytes 1048576 | tf_op jit(solution)/shard_map/all_to_all | solution.py:202
  34.0 36.9 %copy-start.8 = (bf16[4,512,128]{2,1,0:T(8,128)(2,1)}, bf16[4,512,128]{2,1,0:T(8,128)(2,1)S(1)}, u32[]{:S(2)}) copy-start(bf16[4,512,128]{2,1,0:T(8,128)(2,1)S(1)} %pad_maximum_fusion.1.refs_0_) | copy-start | bytes 1572868
  34.0 30.1 %collective-permute-start.14 = (bf16[4,512,128]{2,1,0:T(8,128)(2,1)S(1)}, bf16[4,512,128]{2,1,0:T(8,128)(2,1)S(1)}, u32[]{:S(2)}, u32[]{:S(2)}) collective-permute-start(bf16[4,512,128]{2,1,0:T(8,128)(2,1)S(1)} %pad_maximum_fusion.1.refs_0_), channel_id=1, source_target_pairs={{0,96},{32,0},{64,32},{96,64},{1,97},{33,1},{65,33},{97,65},{2,98}... | collective-permute-start | bytes 1572872 | tf_op jit(solution)/shard_map/ppermute | solution.py:163
  41.7 22.4 %collective-permute-start.13 = (bf16[4,512,128]{2,1,0:T(8,128)(2,1)S(1)}, bf16[4,512,128]{2,1,0:T(8,128)(2,1)S(1)}, u32[]{:S(2)}, u32[]{:S(2)}) collective-permute-start(bf16[4,512,128]{2,1,0:T(8,128)(2,1)S(1)} %pad_maximum_fusion.1.refs_0_), channel_id=1, source_target_pairs={{0,64},{32,96},{64,0},{96,32},{1,65},{33,97},{65,1},{97,33},{2,66}... | collective-permute-start | bytes 1572872 | tf_op jit(solution)/shard_map/ppermute | solution.py:163
  43.6 27.2 %collective-permute-start.12 = (bf16[4,512,128]{2,1,0:T(8,128)(2,1)S(1)}, bf16[4,512,128]{2,1,0:T(8,128)(2,1)S(1)}, u32[]{:S(2)}, u32[]{:S(2)}) collective-permute-start(bf16[4,512,128]{2,1,0:T(8,128)(2,1)S(1)} %pad_maximum_fusion.1.refs_0_), channel_id=1, source_target_pairs={{0,32},{32,64},{64,96},{96,0},{1,33},{33,65},{65,97},{97,1},{2,34}... | collective-permute-start | bytes 1572872 | tf_op jit(solution)/shard_map/ppermute | solution.py:163
  46.8 30.9 %copy-start.13 = (bf16[1,128,1024]{2,1,0:T(8,128)(2,1)S(1)}, bf16[1,128,1024]{2,1,0:T(8,128)(2,1)}, u32[]{:S(2)}) copy-start(bf16[1,128,1024]{2,1,0:T(8,128)(2,1)} %param.12) | copy-start | bytes 786436
  46.8 30.9 %copy-start.14 = (bf16[1,128,1024]{2,1,0:T(8,128)(2,1)S(1)}, bf16[1,128,1024]{2,1,0:T(8,128)(2,1)}, u32[]{:S(2)}) copy-start(bf16[1,128,1024]{2,1,0:T(8,128)(2,1)} %param.11) | copy-start | bytes 786436
  64.1 6.8 %copy-start.9 = (bf16[4,512,128]{2,1,0:T(8,128)(2,1)}, bf16[4,512,128]{2,1,0:T(8,128)(2,1)S(1)}, u32[]{:S(2)}) copy-start(bf16[4,512,128]{2,1,0:T(8,128)(2,1)S(1)} %collective-permute-done.14.refs_3_) | copy-start | bytes 1572868
  64.1 6.8 %copy-start.10 = (bf16[4,512,128]{2,1,0:T(8,128)(2,1)}, bf16[4,512,128]{2,1,0:T(8,128)(2,1)S(1)}, u32[]{:S(2)}) copy-start(bf16[4,512,128]{2,1,0:T(8,128)(2,1)S(1)} %collective-permute-done.13.refs_2_) | copy-start | bytes 1572868
  70.9 0.8 copy-start.11
  75.3 96.0 %collective-permute-start.15 = (bf16[4,512,512]{2,1,0:T(8,128)(2,1)}, bf16[4,512,512]{2,1,0:T(8,128)(2,1)}, u32[]{:S(2)}, u32[]{:S(2)}) collective-permute-start(bf16[4,512,512]{2,1,0:T(8,128)(2,1)} %place.1.refs_4_), channel_id=1, source_target_pairs={{0,16},{16,0},{1,17},{17,1},{2,18},{18,2},{3,19},{19,3},{4,20},{20... | collective-permute-start | bytes 6291464 | tf_op jit(solution)/shard_map/ppermute | solution.py:166
  77.8 21.0 %collective-permute-start.1 = (bf16[2,128,256]{2,1,0:T(8,128)(2,1)S(1)}, bf16[2,128,256]{2,1,0:T(8,128)(2,1)S(1)}, u32[]{:S(2)}, u32[]{:S(2)}) collective-permute-start(bf16[2,128,256]{2,1,0:T(8,128)(2,1)S(1)} %pad_maximum_fusion.4), channel_id=1, source_target_pairs={{0,8},{4,12},{8,0},{12,4},{1,9},{5,13},{9,1},{13,5},{2,10},{6,14},... | collective-permute-start | bytes 393224 | tf_op jit(solution)/shard_map/ppermute | solution.py:187
  89.6 21.9 %collective-permute-start.2 = (bf16[2,128,256]{2,1,0:T(8,128)(2,1)S(1)}, bf16[2,128,256]{2,1,0:T(8,128)(2,1)S(1)}, u32[]{:S(2)}, u32[]{:S(2)}) collective-permute-start(bf16[2,128,256]{2,1,0:T(8,128)(2,1)S(1)} %pad_maximum_fusion.5), channel_id=1, source_target_pairs={{0,12},{4,0},{8,4},{12,8},{1,13},{5,1},{9,5},{13,9},{2,14},{6,2},{... | collective-permute-start | bytes 393224 | tf_op jit(solution)/shard_map/ppermute | solution.py:187
  93.7 17.8 %collective-permute-start = (bf16[2,128,256]{2,1,0:T(8,128)(2,1)S(1)}, bf16[2,128,256]{2,1,0:T(8,128)(2,1)S(1)}, u32[]{:S(2)}, u32[]{:S(2)}) collective-permute-start(bf16[2,128,256]{2,1,0:T(8,128)(2,1)S(1)} %pad_maximum_fusion.3), channel_id=1, source_target_pairs={{0,4},{4,8},{8,12},{12,0},{1,5},{5,9},{9,13},{13,1},{2,6},{6,10},{... | collective-permute-start | bytes 393224 | tf_op jit(solution)/shard_map/ppermute | solution.py:187
  111.8 8.2 %collective-permute-start.5 = (bf16[4,2,128,128]{3,2,1,0:T(8,128)(2,1)S(1)}, bf16[4,2,128,128]{3,2,1,0:T(8,128)(2,1)S(1)}, u32[]{:S(2)}, u32[]{:S(2)}) collective-permute-start(bf16[4,2,128,128]{3,2,1,0:T(8,128)(2,1)S(1)} %get-tuple-element.5), channel_id=1, source_target_pairs={{0,3},{1,0},{2,1},{3,2},{4,7},{5,4},{6,5},{7,6},{8,11},{9,8},{10,9... | collective-permute-start | bytes 786440 | tf_op jit(solution)/shard_map/ppermute | solution.py:195
  113.7 9.2 %collective-permute-start.4 = (bf16[4,2,128,128]{3,2,1,0:T(8,128)(2,1)S(1)}, bf16[4,2,128,128]{3,2,1,0:T(8,128)(2,1)S(1)}, u32[]{:S(2)}, u32[]{:S(2)}) collective-permute-start(bf16[4,2,128,128]{3,2,1,0:T(8,128)(2,1)S(1)} %get-tuple-element.6), channel_id=1, source_target_pairs={{0,2},{1,3},{2,0},{3,1},{4,6},{5,7},{6,4},{7,5},{8,10},{9,11},{10,... | collective-permute-start | bytes 786440 | tf_op jit(solution)/shard_map/ppermute | solution.py:195
  115.6 14.6 %collective-permute-start.3 = (bf16[4,2,128,128]{3,2,1,0:T(8,128)(2,1)S(1)}, bf16[4,2,128,128]{3,2,1,0:T(8,128)(2,1)S(1)}, u32[]{:S(2)}, u32[]{:S(2)}) collective-permute-start(bf16[4,2,128,128]{3,2,1,0:T(8,128)(2,1)S(1)} %get-tuple-element.7), channel_id=1, source_target_pairs={{0,1},{1,2},{2,3},{3,0},{4,5},{5,6},{6,7},{7,4},{8,9},{9,10},{10,1... | collective-permute-start | bytes 786440 | tf_op jit(solution)/shard_map/ppermute | solution.py:195
  120.0 0.7 copy-start.2
  122.9 0.7 copy-start.4
  130.2 0.7 copy-start.6
  130.9 1.0 copy-start.3
  131.9 0.9 copy-start.5
  132.8 0.9 copy-start.7
  133.8 37.5 %copy-start.1 = (bf16[4,512,512]{2,1,0:T(8,128)(2,1)S(1)}, bf16[4,512,512]{2,1,0:T(8,128)(2,1)}, u32[]{:S(2)}) copy-start(bf16[4,512,512]{2,1,0:T(8,128)(2,1)} %place.1.refs_4_) | copy-start | bytes 6291460
  140.8 14.3 %collective-permute-start.8 = (bf16[512,512]{1,0:T(8,128)(2,1)S(1)}, bf16[512,512]{1,0:T(8,128)(2,1)S(1)}, u32[]{:S(2)}, u32[]{:S(2)}) collective-permute-start(bf16[512,512]{1,0:T(8,128)(2,1)S(1)} %attend.1.refs_0_), channel_id=1, source_target_pairs={{0,3},{1,0},{2,1},{3,2},{4,7},{5,4},{6,5},{7,6},{8,11},{9,8},{10,9... | collective-permute-start | bytes 1572872 | tf_op jit(solution)/shard_map/ppermute | solution.py:211
  142.7 15.3 %collective-permute-start.7 = (bf16[512,512]{1,0:T(8,128)(2,1)S(1)}, bf16[512,512]{1,0:T(8,128)(2,1)}, u32[]{:S(2)}, u32[]{:S(2)}) collective-permute-start(bf16[512,512]{1,0:T(8,128)(2,1)S(1)} %attend.1.refs_0_), channel_id=1, source_target_pairs={{0,2},{1,3},{2,0},{3,1},{4,6},{5,7},{6,4},{7,5},{8,10},{9,11},{10,... | collective-permute-start | bytes 1572872 | tf_op jit(solution)/shard_map/ppermute | solution.py:211
  144.7 26.7 %collective-permute-start.6 = (bf16[512,512]{1,0:T(8,128)(2,1)S(1)}, bf16[512,512]{1,0:T(8,128)(2,1)}, u32[]{:S(2)}, u32[]{:S(2)}) collective-permute-start(bf16[512,512]{1,0:T(8,128)(2,1)S(1)} %attend.1.refs_0_), channel_id=1, source_target_pairs={{0,1},{1,2},{2,3},{3,0},{4,5},{5,6},{6,7},{7,4},{8,9},{9,10},{10,1... | collective-permute-start | bytes 1572872 | tf_op jit(solution)/shard_map/ppermute | solution.py:211
  176.5 69.9 %copy-start.12 = (bf16[512,256]{1,0:T(8,128)(2,1)S(1)}, bf16[512,256]{1,0:T(8,128)(2,1)}, u32[]{:S(2)}) copy-start(bf16[512,256]{1,0:T(8,128)(2,1)} %param.15) | copy-start | bytes 786436

commit v2 on v1

--- a/solution.py
+++ b/solution.py
@@ -84,32 +84,6 @@
     )(info, queries, *kv)
 
 
-def place_kernel(where, *refs):
-    parts, (out_ref, held, sems) = refs[:-3], refs[-3:]
-    copies = [pltpu.make_async_copy(part, held.at[t], sems.at[t]) for t, part in enumerate(parts)]
-    for copy in copies:
-        copy.start()
-    for t, copy in enumerate(copies):
-        copy.wait()
-        for s in range(4):
-            out_ref[where[t], :, pl.ds(pl.multiple_of(where[4 + s] * 128, 128), 128)] = held[t, s]
-
-
-def place(where, parts):
-    return pl.pallas_call(
-        place_kernel,
-        out_shape=jax.ShapeDtypeStruct((4, 512, 512), jnp.bfloat16),
-        in_specs=[pl.BlockSpec(memory_space=pltpu.SMEM)] + [pl.BlockSpec(memory_space=pl.ANY)] * len(parts),
-        out_specs=pl.BlockSpec(memory_space=pltpu.VMEM),
-        scratch_shapes=[
-            pltpu.VMEM((len(parts), 4, 512, 128), jnp.bfloat16),
-            pltpu.SemaphoreType.DMA((len(parts),)),
-        ],
-        cost_estimate=pl.CostEstimate(flops=0, transcendentals=0, bytes_accessed=4 << 20),
-        name="place",
-    )(where, *parts)
-
-
 def project_kernel(where, *refs):
     gated, (own_ref, other_any, out_ref, other_ref, sem) = refs[:-5], refs[-5:]
     fetch = pltpu.make_async_copy(other_any, other_ref, sem)
@@ -120,13 +94,17 @@
         if u == 1:
             fetch.wait()
         lanes = pl.ds(pl.multiple_of((c if u == 0 else 1 - c) * 128, 128), 128)
-        for pair in range(2):
-            weight = [w_ref[where[1 + s], :, pair * 256 : (pair + 1) * 256] for s in range(len(gated))]
-            total = jnp.dot(
-                rows, jnp.concatenate(weight, axis=0), preferred_element_type=jnp.float32
-            ).astype(jnp.bfloat16)
-            out_ref[2 * pair, :, lanes] = total[:, :128]
-            out_ref[2 * pair + 1, :, lanes] = total[:, 128:]
+        for pair in (0, 2):
+            weight = jnp.concatenate(
+                [
+                    jnp.concatenate([w_ref[where[1 + s], pair], w_ref[where[1 + s], pair + 1]], axis=1)
+                    for s in range(len(gated))
+                ],
+                axis=0,
+            )
+            total = jnp.dot(rows, weight, preferred_element_type=jnp.float32).astype(jnp.bfloat16)
+            out_ref[where[1 + len(gated)] ^ pair, :, lanes] = total[:, :128]
+            out_ref[where[1 + len(gated)] ^ (pair + 1), :, lanes] = total[:, 128:]
 
 
 def project(where, gated, own, other):
@@ -138,7 +116,7 @@
         out_shape=jax.ShapeDtypeStruct((4, rows, 256), jnp.bfloat16),
         in_specs=[pl.BlockSpec(memory_space=pltpu.SMEM)]
         + [spec] * (parts + 1)
-        + [pl.BlockSpec(memory_space=pl.ANY)],
+        + [pl.BlockSpec(memory_space=pltpu.HBM)],
         out_specs=spec,
         scratch_shapes=[pltpu.VMEM(other.shape, other.dtype), pltpu.SemaphoreType.DMA],
         cost_estimate=pl.CostEstimate(
@@ -153,16 +131,12 @@
     return [(i, (i + by) % size) for i in range(size)]
 
 
-def gather_weight(out_weight, y, zl):
+def gather_weight(out_weight):
     turned = lax.ppermute(out_weight, ("y", "x"), [(y * 4 + x, x * 4 + y) for y in range(4) for x in range(4)])
     pair = jnp.stack([turned, lax.ppermute(turned, "zl", [(i, i ^ 1) for i in range(4)])])
     far = lax.ppermute(pair, "zl", [(i, i ^ 2) for i in range(4)])
     along = jnp.concatenate([pair, far])
-    parts = [along]
-    for s in (1, 2, 3):
-        parts.append(lax.ppermute(along, "y", shifted(4, s)))
-    where = jnp.stack([(y + 4 - t) & 3 for t in range(4)] + [zl ^ s for s in range(4)])
-    own = place(where.astype(jnp.int32), parts)
+    own = lax.all_to_all(jnp.broadcast_to(along[None], (4,) + along.shape), "y", 0, 0, tiled=True)
     other = lax.ppermute(own, "c", [(0, 1), (1, 0)])
     return own, other
 
@@ -195,7 +169,7 @@
         kv_here.append(lax.ppermute(head_for((x + t) & 3), "x", shifted(4, t)))
     block_of = [((zh - s) & 3) * 4 + ((x - t) & 3) for t in range(4) for s in range(4)]
 
-    own, other = gather_weight(out_weight, lax.axis_index("y"), lax.axis_index("zl"))
+    own, other = gather_weight(out_weight)
 
     head_of = first_head + lax.broadcasted_iota(jnp.int32, (1, feature_count), 1) // HD
     marked = jnp.where(ablated[:, None] == head_of, jnp.inf, queries).astype(queries.dtype)
@@ -209,7 +183,8 @@
     gathered = [gated]
     for s in (1, 2, 3):
         gathered.append(lax.ppermute(gated, "x", shifted(4, s)))
-    where = jnp.stack([lax.axis_index("c")] + [(x + 4 - s) & 3 for s in range(4)]).astype(jnp.int32)
+    where = [lax.axis_index("c")] + [(x + 4 - s) & 3 for s in range(4)] + [lax.axis_index("zl")]
+    where = jnp.stack(where).astype(jnp.int32)
     partial = project(where, gathered, own, other)
     partial = partial.reshape(4 * prompts, per_prompt, 256)
     returned = lax.all_to_all(partial, ("zh",) + VAR, 0, 0, tiled=True)

time: 248 us -> 253 us (1.020)
  waiting for transfers between devices: 72.5 us -> 91.7 us
  starting transfers between devices: 77.8 us -> 71.1 us
  blocking collectives: 69.7 us -> 66.9 us
  Pallas kernels: 15.8 us -> 13.2 us
    all_to_all x0 -> x1, waiting for transfers between devices: none -> 24.5 us  [gather_weight(): lax.all_to_all(jnp.broadcast_to(along[None], (4,) + along.shape), 'y', 0,...]
    ppermute x3 -> x0, waiting for transfers between devices: 24.1 us -> none  [gather_weight(): parts.append(lax.ppermute(along, 'y', shifted(4, s)))]
    all_to_all x0 -> x1, starting transfers between devices: none -> 15.1 us  [gather_weight(): lax.all_to_all(jnp.broadcast_to(along[None], (4,) + along.shape), 'y', 0,...]
    ppermute x3 -> x0, starting transfers between devices: 12.1 us -> none  [gather_weight(): parts.append(lax.ppermute(along, 'y', shifted(4, s)))]
    ppermute x1, waiting for transfers between devices: 0.01 us -> 11.5 us  [gather_weight(): far = lax.ppermute(pair, 'zl', [(i, i ^ 2) for i in range(4)])]
    all_to_all x1, starting transfers between devices: 19 us -> 8.3 us  [step(): lax.all_to_all(marked.reshape(prompts, per_prompt, feature_count), VAR, 0...]
    ppermute x3, waiting for transfers between devices: 12.6 us -> 17.9 us  [step(): kv.append(lax.ppermute(heads_for(zh + s & 3), 'zh', shifted(4, s)))]
    pallas_call x1 -> x0, Pallas kernels: 3.64 us -> none  [place(): pl.pallas_call(place_kernel, out_shape=jax.ShapeDtypeStruct((4, 512, 512)...]
  transfers between devices with their start and end apart: 17 -> 15, of which waited for: 9 -> 11; matrix products, arithmetic and copies ran while one was open for 1% -> 1% of each run, Pallas kernels for 4% -> 3%
where the time goes in v2:
time: 253 us; the launch traced here: 252 us
  waiting for transfers between devices  91.7 us (36%)
  starting transfers between devices  71.1 us (28%)
  blocking collectives  66.9 us (26%)
  Pallas kernels  13.2 us (5%)
  local copies, waits for them, and re-layouts  6.49 us (3%)
    all_to_all x1, blocking collectives, step(): returned = lax.all_to_all(partial, ('zh',) + VAR, 0, 0, tiled=True)  66.9 us
    all_to_all x1, waiting for transfers between devices, gather_weight(): lax.all_to_all(jnp.broadcast_to(along[None], (4,) + along.shape), 'y', 0,...  24.5 us
    ppermute x3, waiting for transfers between devices, step(): gathered.append(lax.ppermute(gated, 'x', shifted(4, s)))  23.2 us
    ppermute x3, starting transfers between devices, step(): kv.append(lax.ppermute(heads_for(zh + s & 3), 'zh', shifted(4, s)))  21.7 us
    ppermute x3, waiting for transfers between devices, step(): kv.append(lax.ppermute(heads_for(zh + s & 3), 'zh', shifted(4, s)))  17.9 us
    all_to_all x1, starting transfers between devices, gather_weight(): lax.all_to_all(jnp.broadcast_to(along[None], (4,) + along.shape), 'y', 0,...  15.1 us
    ppermute x1, waiting for transfers between devices, gather_weight(): far = lax.ppermute(pair, 'zl', [(i, i ^ 2) for i in range(4)])  11.5 us
    ppermute x3, waiting for transfers between devices, step(): kv_here.append(lax.ppermute(head_for(x + t & 3), 'x', shifted(4, t)))  10.8 us
  transfers between devices with their start and end apart: 15, of which 11 were waited for; matrix products, arithmetic and copies ran while one was open for 1% of the time, Pallas kernels for 3%

profile of v2, /device:TPU:33, one launch (start us, length us, event | category | flops | bytes accessed | tf_op | source)
XLA Modules:
  0.0 252.4 jit_solution(265617177121527721)
XLA Ops:
  0.0 1.7 collective-permute-start.9
  1.7 0.0 collective-permute-done.9
  1.7 1.9 collective-permute-start.10
  3.6 3.8 %collective-permute-done.10 = bf16[512,128]{1,0:T(8,128)(2,1)S(1)} collective-permute-done((bf16[512,128]{1,0:T(8,128)(2,1)S(1)}, bf16[512,128]{1,0:T(8,128)(2,1)S(1)}, u32[]{:S(2)}, u32[]{:S(2)}) %collective-permute-start.10) | collective-permute-done | bytes 131104 | tf_op jit(solution)/shard_map/ppermute | solution.py:136
  7.4 5.5 %collective-permute-start.11 = (bf16[2,512,128]{2,1,0:T(8,128)(2,1)S(1)}, bf16[2,512,128]{2,1,0:T(8,128)(2,1)S(1)}, u32[]{:S(2)}, u32[]{:S(2)}) collective-permute-start(bf16[2,512,128]{2,1,0:T(8,128)(2,1)S(1)} %pad_maximum_fusion.2), channel_id=1, source_target_pairs={{0,256},{128,384},{256,0},{384,128},{1,257},{129,385},{257,1},{385... | collective-permute-start | bytes 786440 | tf_op jit(solution)/shard_map/ppermute | solution.py:137
  12.9 11.5 %collective-permute-done.11 = bf16[2,512,128]{2,1,0:T(8,128)(2,1)S(1)} collective-permute-done((bf16[2,512,128]{2,1,0:T(8,128)(2,1)S(1)}, bf16[2,512,128]{2,1,0:T(8,128)(2,1)S(1)}, u32[]{:S(2)}, u32[]{:S(2)}) %collective-permute-start.11) | collective-permute-done | bytes 262176 | tf_op jit(solution)/shard_map/ppermute | solution.py:137
  24.4 0.1 pad_maximum_fusion.1
  24.5 1.7 broadcast_in_dim.12
  26.2 15.1 %all-to-all-start.1 = ((bf16[4,4,512,128]{3,2,1,0:T(8,128)(2,1)}), bf16[4,4,512,128]{3,2,1,0:T(8,128)(2,1)S(1)}, u32[]{:S(2)}, u32[]{:S(2)}) async-start(bf16[4,4,512,128]{3,2,1,0:T(8,128)(2,1)} %broadcast_in_dim.12), calls=%async_computation.1 | async-start | bytes 4194304 | tf_op jit(solution)/shard_map/all_to_all | solution.py:139
  41.4 1.0 compare_select_fusion
  42.3 24.5 %all-to-all-done.1.refs_4_ = bf16[4,4,512,128]{3,2,1,0:T(8,128)(2,1)S(1)} async-done(((bf16[4,4,512,128]{3,2,1,0:T(8,128)(2,1)}), bf16[4,4,512,128]{3,2,1,0:T(8,128)(2,1)S(1)}, u32[]{:S(2)}, u32[]{:S(2)}) %all-to-all-start.1) | async-done | bytes 2097184 | tf_op jit(solution)/shard_map/all_to_all | solution.py:139
  66.8 8.3 %all-to-all-start = ((bf16[32,16,512]{2,1,0:T(8,128)(2,1)}), bf16[32,16,512]{2,1,0:T(8,128)(2,1)S(1)}, u32[]{:S(2)}, u32[]{:S(2)}) async-start(bf16[32,16,512]{2,1,0:T(8,128)(2,1)} %bitcast.22), calls=%async_computation | async-start | bytes 1048576 | tf_op jit(solution)/shard_map/all_to_all | solution.py:176
  75.1 2.3 collective-permute-start.12
  77.4 0.1 constant_dynamic-slice_fusion.10
  77.6 12.5 %collective-permute-start.1 = (bf16[2,128,256]{2,1,0:T(8,128)(2,1)S(1)}, bf16[2,128,256]{2,1,0:T(8,128)(2,1)S(1)}, u32[]{:S(2)}, u32[]{:S(2)}) collective-permute-start(bf16[2,128,256]{2,1,0:T(8,128)(2,1)S(1)} %pad_maximum_fusion.4), channel_id=1, source_target_pairs={{0,8},{4,12},{8,0},{12,4},{1,9},{5,13},{9,1},{13,5},{2,10},{6,14},... | collective-permute-start | bytes 393224 | tf_op jit(solution)/shard_map/ppermute | solution.py:161
  90.1 3.3 %collective-permute-start.2 = (bf16[2,128,256]{2,1,0:T(8,128)(2,1)S(1)}, bf16[2,128,256]{2,1,0:T(8,128)(2,1)S(1)}, u32[]{:S(2)}, u32[]{:S(2)}) collective-permute-start(bf16[2,128,256]{2,1,0:T(8,128)(2,1)S(1)} %pad_maximum_fusion.5), channel_id=1, source_target_pairs={{0,12},{4,0},{8,4},{12,8},{1,13},{5,1},{9,5},{13,9},{2,14},{6,2},{... | collective-permute-start | bytes 393224 | tf_op jit(solution)/shard_map/ppermute | solution.py:161
  93.4 5.9 %collective-permute-start = (bf16[2,128,256]{2,1,0:T(8,128)(2,1)S(1)}, bf16[2,128,256]{2,1,0:T(8,128)(2,1)S(1)}, u32[]{:S(2)}, u32[]{:S(2)}) collective-permute-start(bf16[2,128,256]{2,1,0:T(8,128)(2,1)S(1)} %pad_maximum_fusion.3), channel_id=1, source_target_pairs={{0,4},{4,8},{8,12},{12,0},{1,5},{5,9},{9,13},{13,1},{2,6},{6,10},{... | collective-permute-start | bytes 393224 | tf_op jit(solution)/shard_map/ppermute | solution.py:161
  99.3 0.0 collective-permute-done.1
  99.3 6.5 %collective-permute-done.2 = bf16[2,128,256]{2,1,0:T(8,128)(2,1)S(1)} collective-permute-done((bf16[2,128,256]{2,1,0:T(8,128)(2,1)S(1)}, bf16[2,128,256]{2,1,0:T(8,128)(2,1)S(1)}, u32[]{:S(2)}, u32[]{:S(2)}) %collective-permute-start.2) | collective-permute-done | bytes 131104 | tf_op jit(solution)/shard_map/ppermute | solution.py:161
  105.8 11.5 %collective-permute-done = bf16[2,128,256]{2,1,0:T(8,128)(2,1)S(1)} collective-permute-done((bf16[2,128,256]{2,1,0:T(8,128)(2,1)S(1)}, bf16[2,128,256]{2,1,0:T(8,128)(2,1)S(1)}, u32[]{:S(2)}, u32[]{:S(2)}) %collective-permute-start) | collective-permute-done | bytes 131104 | tf_op jit(solution)/shard_map/ppermute | solution.py:161
  117.3 0.1 pad_maximum_fusion
  117.4 1.0 constant_dynamic-slice_fusion
  118.3 3.0 %collective-permute-start.5 = (bf16[4,2,128,128]{3,2,1,0:T(8,128)(2,1)}, bf16[4,2,128,128]{3,2,1,0:T(8,128)(2,1)S(1)}, u32[]{:S(2)}, u32[]{:S(2)}) collective-permute-start(bf16[4,2,128,128]{3,2,1,0:T(8,128)(2,1)} %get-tuple-element.5), channel_id=1, source_target_pairs={{0,3},{1,0},{2,1},{3,2},{4,7},{5,4},{6,5},{7,6},{8,11},{9,8},{10,9... | collective-permute-start | bytes 786440 | tf_op jit(solution)/shard_map/ppermute | solution.py:169
  121.4 1.9 collective-permute-start.4
  123.3 2.5 collective-permute-start.3
  126.5 0.2 fusion.1
  126.7 0.1 concatenate.7.info
  126.8 0.8 collective-permute-done.5.refs_3_
  127.6 0.7 copy-done.1
  128.3 3.6 %collective-permute-done.4.refs_2_ = bf16[4,2,128,128]{3,2,1,0:T(8,128)(2,1)S(1)} collective-permute-done((bf16[4,2,128,128]{3,2,1,0:T(8,128)(2,1)}, bf16[4,2,128,128]{3,2,1,0:T(8,128)(2,1)S(1)}, u32[]{:S(2)}, u32[]{:S(2)}) %collective-permute-start.4) | collective-permute-done | bytes 262176 | tf_op jit(solution)/shard_map/ppermute | solution.py:169
  132.0 0.7 copy-done.3
  132.7 6.3 %collective-permute-done.3.refs_1_ = bf16[4,2,128,128]{3,2,1,0:T(8,128)(2,1)} collective-permute-done((bf16[4,2,128,128]{3,2,1,0:T(8,128)(2,1)}, bf16[4,2,128,128]{3,2,1,0:T(8,128)(2,1)}, u32[]{:S(2)}, u32[]{:S(2)}) %collective-permute-start.3) | collective-permute-done | bytes 262176 | tf_op jit(solution)/shard_map/ppermute | solution.py:169
  138.9 0.0 all-to-all-done
  139.0 0.9 copy-done.2
  139.9 0.9 copy-done.4
  140.9 8.0 %attend.1.refs_0_ = bf16[512,512]{1,0:T(8,128)(2,1)S(1)} custom-call(s32[21]{0:T(128)S(1)} %concatenate.7.info, bf16[512,512]{1,0:T(8,128)(2,1)S(1)} %bitcast.36, bf16[4,2,128,128]{3,2,1,0:T(8,128)(2,1)S(1)} %get-tuple-element.8.refs_0_, bf16[4,2,128,128]{3,2,1,0:T(8,128)(2,1)} %collective-permute-done.3.refs_1_, bf16[4,2,128,128]{3,2,1,0:T(8,128)(2,1)S(1)} %copy-done.4, ...), custom_call_target="tpu_custom_call" | custom-call | flops 2147483648 | bytes 2097152 | tf_op jit(solution)/shard_map/attend/pallas_call | solution.py:63
  148.8 1.9 collective-permute-start.8
  150.7 1.9 collective-permute-start.7
  152.7 3.4 %collective-permute-start.6 = (bf16[512,512]{1,0:T(8,128)(2,1)S(1)}, bf16[512,512]{1,0:T(8,128)(2,1)}, u32[]{:S(2)}, u32[]{:S(2)}) collective-permute-start(bf16[512,512]{1,0:T(8,128)(2,1)S(1)} %attend.1.refs_0_), channel_id=1, source_target_pairs={{0,1},{1,2},{2,3},{3,0},{4,5},{5,6},{6,7},{7,4},{8,9},{9,10},{10,1... | collective-permute-start | bytes 1572872 | tf_op jit(solution)/shard_map/ppermute | solution.py:185
  156.0 0.1 stack.119.where
  156.1 7.7 %collective-permute-done.8.refs_3_ = bf16[512,512]{1,0:T(8,128)(2,1)S(1)} collective-permute-done((bf16[512,512]{1,0:T(8,128)(2,1)S(1)}, bf16[512,512]{1,0:T(8,128)(2,1)S(1)}, u32[]{:S(2)}, u32[]{:S(2)}) %collective-permute-start.8) | collective-permute-done | bytes 524320 | tf_op jit(solution)/shard_map/ppermute | solution.py:185
  163.8 2.9 %collective-permute-done.7.refs_2_ = bf16[512,512]{1,0:T(8,128)(2,1)} collective-permute-done((bf16[512,512]{1,0:T(8,128)(2,1)S(1)}, bf16[512,512]{1,0:T(8,128)(2,1)}, u32[]{:S(2)}, u32[]{:S(2)}) %collective-permute-start.7) | collective-permute-done | bytes 524320 | tf_op jit(solution)/shard_map/ppermute | solution.py:185
  166.7 12.6 %collective-permute-done.6.refs_1_ = bf16[512,512]{1,0:T(8,128)(2,1)} collective-permute-done((bf16[512,512]{1,0:T(8,128)(2,1)S(1)}, bf16[512,512]{1,0:T(8,128)(2,1)}, u32[]{:S(2)}, u32[]{:S(2)}) %collective-permute-start.6) | collective-permute-done | bytes 524320 | tf_op jit(solution)/shard_map/ppermute | solution.py:185
  179.3 5.3 %project.1 = bf16[4,512,256]{2,1,0:T(8,128)(2,1)S(1)} custom-call(s32[6]{0:T(128)S(1)} %stack.119.where, bf16[512,512]{1,0:T(8,128)(2,1)S(1)} %attend.1.refs_0_, bf16[512,512]{1,0:T(8,128)(2,1)} %collective-permute-done.6.refs_1_, bf16[512,512]{1,0:T(8,128)(2,1)} %collective-permute-done.7.refs_2_, bf16[512,512]{1,0:T(8,128)(2,1)S(1)} %collective-permute-done.8.refs_3_, ...), custom_call_target="tpu_custom_call" | custom-call | flops 2147483648 | bytes 8388608 | tf_op jit(solution)/shard_map/project/pallas_call | solution.py:114
  184.6 0.0 copy-start.6
  184.6 66.9 %all_to_all.15 = bf16[128,16,256]{2,1,0:T(8,128)(2,1)S(1)} all-to-all(bf16[128,16,256]{2,1,0:T(8,128)(2,1)S(1)} %bitcast.35), channel_id=1, replica_groups=mesh['zl'=4,'y'=4,'c'=2,'zh'=4,'x'=4] {'zh','zl','y','c'}, dimensions={0} | all-to-all | bytes 2097152 | tf_op jit(solution)/shard_map/all_to_all | solution.py:190
  251.5 0.1 bitcast_reduce_fusion
  251.7 0.8 add_convert_fusion
  (22 shorter events, 0.1 us)
Async XLA Ops:
  0.0 126.5 %copy-start = (s32[32,4]{0,1:T(4,128)S(1)}, s32[32,4]{0,1:T(4,128)}, u32[]{:S(2)}) copy-start(s32[32,4]{0,1:T(4,128)} %param.10) | copy-start | bytes 1540
  0.0 1.7 collective-permute-start.9
  1.7 5.7 %collective-permute-start.10 = (bf16[512,128]{1,0:T(8,128)(2,1)S(1)}, bf16[512,128]{1,0:T(8,128)(2,1)S(1)}, u32[]{:S(2)}, u32[]{:S(2)}) collective-permute-start(bf16[512,128]{1,0:T(8,128)(2,1)S(1)} %collective-permute-done.9), channel_id=1, source_target_pairs={{0,128},{128,0},{256,384},{384,256},{1,129},{129,1},{257,385},{385... | collective-permute-start | bytes 393224 | tf_op jit(solution)/shard_map/ppermute | solution.py:136
  7.4 17.0 %collective-permute-start.11 = (bf16[2,512,128]{2,1,0:T(8,128)(2,1)S(1)}, bf16[2,512,128]{2,1,0:T(8,128)(2,1)S(1)}, u32[]{:S(2)}, u32[]{:S(2)}) collective-permute-start(bf16[2,512,128]{2,1,0:T(8,128)(2,1)S(1)} %pad_maximum_fusion.2), channel_id=1, source_target_pairs={{0,256},{128,384},{256,0},{384,128},{1,257},{129,385},{257,1},{385... | collective-permute-start | bytes 786440 | tf_op jit(solution)/shard_map/ppermute | solution.py:137
  26.2 15.1 %copy-start.5 = (bf16[512,512]{1,0:T(8,128)(2,1)S(1)}, bf16[512,512]{1,0:T(8,128)(2,1)}, u32[]{:S(2)}) copy-start(bf16[512,512]{1,0:T(8,128)(2,1)} %param.8) | copy-start | bytes 1572868
  26.2 15.1 %copy-start.9 = (s32[512]{0:T(512)S(1)}, s32[512]{0:T(512)}, u32[]{:S(2)}) copy-start(s32[512]{0:T(512)} %param.9) | copy-start | bytes 6148
  26.2 40.6 %all-to-all-start.1 = ((bf16[4,4,512,128]{3,2,1,0:T(8,128)(2,1)}), bf16[4,4,512,128]{3,2,1,0:T(8,128)(2,1)S(1)}, u32[]{:S(2)}, u32[]{:S(2)}) async-start(bf16[4,4,512,128]{3,2,1,0:T(8,128)(2,1)} %broadcast_in_dim.12), calls=%async_computation.1 | async-start | bytes 4194304 | tf_op jit(solution)/shard_map/all_to_all | solution.py:139
  41.3 36.1 %copy-start.7 = (bf16[1,128,1024]{2,1,0:T(8,128)(2,1)S(1)}, bf16[1,128,1024]{2,1,0:T(8,128)(2,1)}, u32[]{:S(2)}) copy-start(bf16[1,128,1024]{2,1,0:T(8,128)(2,1)} %param.12) | copy-start | bytes 786436
  41.3 36.1 %copy-start.8 = (bf16[1,128,1024]{2,1,0:T(8,128)(2,1)S(1)}, bf16[1,128,1024]{2,1,0:T(8,128)(2,1)}, u32[]{:S(2)}) copy-start(bf16[1,128,1024]{2,1,0:T(8,128)(2,1)} %param.11) | copy-start | bytes 786436
  66.8 72.2 %all-to-all-start = ((bf16[32,16,512]{2,1,0:T(8,128)(2,1)}), bf16[32,16,512]{2,1,0:T(8,128)(2,1)S(1)}, u32[]{:S(2)}, u32[]{:S(2)}) async-start(bf16[32,16,512]{2,1,0:T(8,128)(2,1)} %bitcast.22), calls=%async_computation | async-start | bytes 1048576 | tf_op jit(solution)/shard_map/all_to_all | solution.py:176
  75.1 104.2 %collective-permute-start.12 = (bf16[4,4,512,128]{3,2,1,0:T(8,128)(2,1)S(1)}, bf16[4,4,512,128]{3,2,1,0:T(8,128)(2,1)}, u32[]{:S(2)}, u32[]{:S(2)}) collective-permute-start(bf16[4,4,512,128]{3,2,1,0:T(8,128)(2,1)S(1)} %all-to-all-done.1.refs_4_), channel_id=1, source_target_pairs={{0,16},{16,0},{1,17},{17,1},{2,18},{18,2},{3,19},{19,3},{4,20},{20... | collective-permute-start | bytes 6291464 | tf_op jit(solution)/shard_map/ppermute | solution.py:140
  77.6 21.8 %collective-permute-start.1 = (bf16[2,128,256]{2,1,0:T(8,128)(2,1)S(1)}, bf16[2,128,256]{2,1,0:T(8,128)(2,1)S(1)}, u32[]{:S(2)}, u32[]{:S(2)}) collective-permute-start(bf16[2,128,256]{2,1,0:T(8,128)(2,1)S(1)} %pad_maximum_fusion.4), channel_id=1, source_target_pairs={{0,8},{4,12},{8,0},{12,4},{1,9},{5,13},{9,1},{13,5},{2,10},{6,14},... | collective-permute-start | bytes 393224 | tf_op jit(solution)/shard_map/ppermute | solution.py:161
  90.1 15.8 %collective-permute-start.2 = (bf16[2,128,256]{2,1,0:T(8,128)(2,1)S(1)}, bf16[2,128,256]{2,1,0:T(8,128)(2,1)S(1)}, u32[]{:S(2)}, u32[]{:S(2)}) collective-permute-start(bf16[2,128,256]{2,1,0:T(8,128)(2,1)S(1)} %pad_maximum_fusion.5), channel_id=1, source_target_pairs={{0,12},{4,0},{8,4},{12,8},{1,13},{5,1},{9,5},{13,9},{2,14},{6,2},{... | collective-permute-start | bytes 393224 | tf_op jit(solution)/shard_map/ppermute | solution.py:161
  93.4 23.9 %collective-permute-start = (bf16[2,128,256]{2,1,0:T(8,128)(2,1)S(1)}, bf16[2,128,256]{2,1,0:T(8,128)(2,1)S(1)}, u32[]{:S(2)}, u32[]{:S(2)}) collective-permute-start(bf16[2,128,256]{2,1,0:T(8,128)(2,1)S(1)} %pad_maximum_fusion.3), channel_id=1, source_target_pairs={{0,4},{4,8},{8,12},{12,0},{1,5},{5,9},{9,13},{13,1},{2,6},{6,10},{... | collective-permute-start | bytes 393224 | tf_op jit(solution)/shard_map/ppermute | solution.py:161
  118.3 9.3 %collective-permute-start.5 = (bf16[4,2,128,128]{3,2,1,0:T(8,128)(2,1)}, bf16[4,2,128,128]{3,2,1,0:T(8,128)(2,1)S(1)}, u32[]{:S(2)}, u32[]{:S(2)}) collective-permute-start(bf16[4,2,128,128]{3,2,1,0:T(8,128)(2,1)} %get-tuple-element.5), channel_id=1, source_target_pairs={{0,3},{1,0},{2,1},{3,2},{4,7},{5,4},{6,5},{7,6},{8,11},{9,8},{10,9... | collective-permute-start | bytes 786440 | tf_op jit(solution)/shard_map/ppermute | solution.py:169
  121.4 10.6 %collective-permute-start.4 = (bf16[4,2,128,128]{3,2,1,0:T(8,128)(2,1)}, bf16[4,2,128,128]{3,2,1,0:T(8,128)(2,1)S(1)}, u32[]{:S(2)}, u32[]{:S(2)}) collective-permute-start(bf16[4,2,128,128]{3,2,1,0:T(8,128)(2,1)} %get-tuple-element.6), channel_id=1, source_target_pairs={{0,2},{1,3},{2,0},{3,1},{4,6},{5,7},{6,4},{7,5},{8,10},{9,11},{10,... | collective-permute-start | bytes 786440 | tf_op jit(solution)/shard_map/ppermute | solution.py:169
  123.3 15.6 %collective-permute-start.3 = (bf16[4,2,128,128]{3,2,1,0:T(8,128)(2,1)}, bf16[4,2,128,128]{3,2,1,0:T(8,128)(2,1)}, u32[]{:S(2)}, u32[]{:S(2)}) collective-permute-start(bf16[4,2,128,128]{3,2,1,0:T(8,128)(2,1)} %get-tuple-element.7), channel_id=1, source_target_pairs={{0,1},{1,2},{2,3},{3,0},{4,5},{5,6},{6,7},{7,4},{8,9},{9,10},{10,1... | collective-permute-start | bytes 786440 | tf_op jit(solution)/shard_map/ppermute | solution.py:169
  127.6 0.7 copy-start.1
  132.0 0.7 copy-start.3
  138.9 1.0 copy-start.2
  139.9 0.9 copy-start.4
  148.8 15.0 %collective-permute-start.8 = (bf16[512,512]{1,0:T(8,128)(2,1)S(1)}, bf16[512,512]{1,0:T(8,128)(2,1)S(1)}, u32[]{:S(2)}, u32[]{:S(2)}) collective-permute-start(bf16[512,512]{1,0:T(8,128)(2,1)S(1)} %attend.1.refs_0_), channel_id=1, source_target_pairs={{0,3},{1,0},{2,1},{3,2},{4,7},{5,4},{6,5},{7,6},{8,11},{9,8},{10,9... | collective-permute-start | bytes 1572872 | tf_op jit(solution)/shard_map/ppermute | solution.py:185
  150.7 15.9 %collective-permute-start.7 = (bf16[512,512]{1,0:T(8,128)(2,1)S(1)}, bf16[512,512]{1,0:T(8,128)(2,1)}, u32[]{:S(2)}, u32[]{:S(2)}) collective-permute-start(bf16[512,512]{1,0:T(8,128)(2,1)S(1)} %attend.1.refs_0_), channel_id=1, source_target_pairs={{0,2},{1,3},{2,0},{3,1},{4,6},{5,7},{6,4},{7,5},{8,10},{9,11},{10,... | collective-permute-start | bytes 1572872 | tf_op jit(solution)/shard_map/ppermute | solution.py:185
  152.7 26.7 %collective-permute-start.6 = (bf16[512,512]{1,0:T(8,128)(2,1)S(1)}, bf16[512,512]{1,0:T(8,128)(2,1)}, u32[]{:S(2)}, u32[]{:S(2)}) collective-permute-start(bf16[512,512]{1,0:T(8,128)(2,1)S(1)} %attend.1.refs_0_), channel_id=1, source_target_pairs={{0,1},{1,2},{2,3},{3,0},{4,5},{5,6},{6,7},{7,4},{8,9},{9,10},{10,1... | collective-permute-start | bytes 1572872 | tf_op jit(solution)/shard_map/ppermute | solution.py:185
  184.6 67.0 %copy-start.6 = (bf16[512,256]{1,0:T(8,128)(2,1)S(1)}, bf16[512,256]{1,0:T(8,128)(2,1)}, u32[]{:S(2)}) copy-start(bf16[512,256]{1,0:T(8,128)(2,1)} %param.15) | copy-start | bytes 786436

commit v3 on v2

--- a/solution.py
+++ b/solution.py
@@ -173,8 +173,9 @@
 
     head_of = first_head + lax.broadcasted_iota(jnp.int32, (1, feature_count), 1) // HD
     marked = jnp.where(ablated[:, None] == head_of, jnp.inf, queries).astype(queries.dtype)
+    rows = marked.reshape(4, prompts // 4, per_prompt, feature_count).transpose(1, 0, 2, 3)
     arrived = lax.all_to_all(
-        marked.reshape(prompts, per_prompt, feature_count), VAR, 0, 0, tiled=True
+        rows.reshape(prompts, per_prompt, feature_count), ("y", "c", "zl"), 0, 0, tiled=True
     ).reshape(row_count, feature_count)
 
     keep = lax.dynamic_index_in_dim(head_keep, var_position, 0, keepdims=False)
@@ -187,9 +188,10 @@
     where = jnp.stack(where).astype(jnp.int32)
     partial = project(where, gathered, own, other)
     partial = partial.reshape(4 * prompts, per_prompt, 256)
-    returned = lax.all_to_all(partial, ("zh",) + VAR, 0, 0, tiled=True)
+    returned = lax.all_to_all(partial, ("zh", "y", "c", "zl"), 0, 0, tiled=True)
     projected = jnp.sum(returned.reshape(4, row_count, 256).astype(jnp.float32), axis=0)
-    projected = projected.astype(jnp.bfloat16)
+    projected = projected.astype(jnp.bfloat16).reshape(prompts // 4, 4, per_prompt, 256)
+    projected = projected.transpose(1, 0, 2, 3).reshape(row_count, 256)
     return (residual.astype(jnp.float32) + projected.astype(jnp.float32)).astype(jnp.bfloat16)
 
 

time: 253 us -> 255 us (level)
  the two profiles are of different devices: /device:TPU:33 before, /device:TPU:24 now
where the time goes in v3:
time: 255 us; the launch traced here: 254 us
  waiting for transfers between devices  92.7 us (36%)
  blocking collectives  71.1 us (28%)
  starting transfers between devices  66.2 us (26%)
  Pallas kernels  13.2 us (5%)
  local copies, waits for them, and re-layouts  8.05 us (3%)
    all_to_all x1, blocking collectives, step(): returned = lax.all_to_all(partial, ('zh', 'y', 'c', 'zl'), 0, 0, tiled=True)  71.1 us
    all_to_all x1, waiting for transfers between devices, gather_weight(): lax.all_to_all(jnp.broadcast_to(along[None], (4,) + along.shape), 'y', 0,...  22.7 us
    ppermute x3, waiting for transfers between devices, step(): gathered.append(lax.ppermute(gated, 'x', shifted(4, s)))  22.6 us
    ppermute x3, starting transfers between devices, step(): kv.append(lax.ppermute(heads_for(zh + s & 3), 'zh', shifted(4, s)))  22.5 us
    ppermute x3, waiting for transfers between devices, step(): kv.append(lax.ppermute(heads_for(zh + s & 3), 'zh', shifted(4, s)))  14 us
    ppermute x1, waiting for transfers between devices, gather_weight(): far = lax.ppermute(pair, 'zl', [(i, i ^ 2) for i in range(4)])  10.9 us
    ppermute x3, waiting for transfers between devices, step(): kv_here.append(lax.ppermute(head_for(x + t & 3), 'x', shifted(4, t)))  10.2 us
    ppermute x1, waiting for transfers between devices, gather_weight(): lax.ppermute(out_weight, ('y', 'x'), [(y * 4 + x, x * 4 + y) for y in ran...  9.14 us
  transfers between devices with their start and end apart: 15, of which 11 were waited for; matrix products, arithmetic and copies ran while one was open for 1% of the time, Pallas kernels for 3%

profile of v3, /device:TPU:24, one launch (start us, length us, event | category | flops | bytes accessed | tf_op | source)
XLA Modules:
  0.0 253.7 jit_solution(14606883406329340112)
XLA Ops:
  0.0 4.4 %collective-permute-start.9 = (bf16[512,128]{1,0:T(8,128)(2,1)}, bf16[512,128]{1,0:T(8,128)(2,1)S(1)}, u32[]{:S(2)}, u32[]{:S(2)}) collective-permute-start(bf16[512,128]{1,0:T(8,128)(2,1)} %param.14), channel_id=1, source_target_pairs={{0,0},{1,32},{2,64},{3,96},{32,1},{33,33},{34,65},{35,97},{64,2},{... | collective-permute-start | bytes 393224 | tf_op jit(solution)/shard_map/ppermute | solution.py:135
  4.5 9.1 %collective-permute-done.9 = bf16[512,128]{1,0:T(8,128)(2,1)S(1)} collective-permute-done((bf16[512,128]{1,0:T(8,128)(2,1)}, bf16[512,128]{1,0:T(8,128)(2,1)S(1)}, u32[]{:S(2)}, u32[]{:S(2)}) %collective-permute-start.9) | collective-permute-done | bytes 131104 | tf_op jit(solution)/shard_map/ppermute | solution.py:135
  13.6 3.8 %collective-permute-start.10 = (bf16[512,128]{1,0:T(8,128)(2,1)S(1)}, bf16[512,128]{1,0:T(8,128)(2,1)S(1)}, u32[]{:S(2)}, u32[]{:S(2)}) collective-permute-start(bf16[512,128]{1,0:T(8,128)(2,1)S(1)} %collective-permute-done.9), channel_id=1, source_target_pairs={{0,128},{128,0},{256,384},{384,256},{1,129},{129,1},{257,385},{385... | collective-permute-start | bytes 393224 | tf_op jit(solution)/shard_map/ppermute | solution.py:136
  17.4 3.2 %collective-permute-done.10 = bf16[512,128]{1,0:T(8,128)(2,1)S(1)} collective-permute-done((bf16[512,128]{1,0:T(8,128)(2,1)S(1)}, bf16[512,128]{1,0:T(8,128)(2,1)S(1)}, u32[]{:S(2)}, u32[]{:S(2)}) %collective-permute-start.10) | collective-permute-done | bytes 131104 | tf_op jit(solution)/shard_map/ppermute | solution.py:136
  20.6 5.2 %collective-permute-start.11 = (bf16[2,512,128]{2,1,0:T(8,128)(2,1)S(1)}, bf16[2,512,128]{2,1,0:T(8,128)(2,1)S(1)}, u32[]{:S(2)}, u32[]{:S(2)}) collective-permute-start(bf16[2,512,128]{2,1,0:T(8,128)(2,1)S(1)} %pad_maximum_fusion.2), channel_id=1, source_target_pairs={{0,256},{128,384},{256,0},{384,128},{1,257},{129,385},{257,1},{385... | collective-permute-start | bytes 786440 | tf_op jit(solution)/shard_map/ppermute | solution.py:137
  25.8 10.9 %collective-permute-done.11 = bf16[2,512,128]{2,1,0:T(8,128)(2,1)S(1)} collective-permute-done((bf16[2,512,128]{2,1,0:T(8,128)(2,1)S(1)}, bf16[2,512,128]{2,1,0:T(8,128)(2,1)S(1)}, u32[]{:S(2)}, u32[]{:S(2)}) %collective-permute-start.11) | collective-permute-done | bytes 262176 | tf_op jit(solution)/shard_map/ppermute | solution.py:137
  36.8 0.1 pad_maximum_fusion.1
  36.8 1.7 broadcast_in_dim.12
  38.6 4.6 %all-to-all-start.1 = ((bf16[4,4,512,128]{3,2,1,0:T(8,128)(2,1)}), bf16[4,4,512,128]{3,2,1,0:T(8,128)(2,1)S(1)}, u32[]{:S(2)}, u32[]{:S(2)}) async-start(bf16[4,4,512,128]{3,2,1,0:T(8,128)(2,1)} %broadcast_in_dim.12), calls=%async_computation.1 | async-start | bytes 4194304 | tf_op jit(solution)/shard_map/all_to_all | solution.py:139
  43.2 0.2 compare_select_fusion
  43.4 0.8 copy.11
  44.3 22.7 %all-to-all-done.1.refs_4_ = bf16[4,4,512,128]{3,2,1,0:T(8,128)(2,1)S(1)} async-done(((bf16[4,4,512,128]{3,2,1,0:T(8,128)(2,1)}), bf16[4,4,512,128]{3,2,1,0:T(8,128)(2,1)S(1)}, u32[]{:S(2)}, u32[]{:S(2)}) %all-to-all-start.1) | async-done | bytes 2097184 | tf_op jit(solution)/shard_map/all_to_all | solution.py:139
  66.9 8.0 %all-to-all-start = ((bf16[32,16,512]{2,1,0:T(8,128)(2,1)}), bf16[32,16,512]{2,1,0:T(8,128)(2,1)S(1)}, u32[]{:S(2)}, u32[]{:S(2)}) async-start(bf16[32,16,512]{2,1,0:T(8,128)(2,1)} %bitcast.24), calls=%async_computation | async-start | bytes 1048576 | tf_op jit(solution)/shard_map/all_to_all | solution.py:177
  75.0 2.1 collective-permute-start.12
  77.1 0.1 constant_dynamic-slice_fusion.10
  77.2 12.8 %collective-permute-start.1 = (bf16[2,128,256]{2,1,0:T(8,128)(2,1)S(1)}, bf16[2,128,256]{2,1,0:T(8,128)(2,1)S(1)}, u32[]{:S(2)}, u32[]{:S(2)}) collective-permute-start(bf16[2,128,256]{2,1,0:T(8,128)(2,1)S(1)} %pad_maximum_fusion.4), channel_id=1, source_target_pairs={{0,8},{4,12},{8,0},{12,4},{1,9},{5,13},{9,1},{13,5},{2,10},{6,14},... | collective-permute-start | bytes 393224 | tf_op jit(solution)/shard_map/ppermute | solution.py:161
  90.0 3.6 %collective-permute-start.2 = (bf16[2,128,256]{2,1,0:T(8,128)(2,1)S(1)}, bf16[2,128,256]{2,1,0:T(8,128)(2,1)S(1)}, u32[]{:S(2)}, u32[]{:S(2)}) collective-permute-start(bf16[2,128,256]{2,1,0:T(8,128)(2,1)S(1)} %pad_maximum_fusion.5), channel_id=1, source_target_pairs={{0,12},{4,0},{8,4},{12,8},{1,13},{5,1},{9,5},{13,9},{2,14},{6,2},{... | collective-permute-start | bytes 393224 | tf_op jit(solution)/shard_map/ppermute | solution.py:161
  93.6 6.1 %collective-permute-start = (bf16[2,128,256]{2,1,0:T(8,128)(2,1)S(1)}, bf16[2,128,256]{2,1,0:T(8,128)(2,1)S(1)}, u32[]{:S(2)}, u32[]{:S(2)}) collective-permute-start(bf16[2,128,256]{2,1,0:T(8,128)(2,1)S(1)} %pad_maximum_fusion.3), channel_id=1, source_target_pairs={{0,4},{4,8},{8,12},{12,0},{1,5},{5,9},{9,13},{13,1},{2,6},{6,10},{... | collective-permute-start | bytes 393224 | tf_op jit(solution)/shard_map/ppermute | solution.py:161
  99.8 14.0 %collective-permute-done.2 = bf16[2,128,256]{2,1,0:T(8,128)(2,1)S(1)} collective-permute-done((bf16[2,128,256]{2,1,0:T(8,128)(2,1)S(1)}, bf16[2,128,256]{2,1,0:T(8,128)(2,1)S(1)}, u32[]{:S(2)}, u32[]{:S(2)}) %collective-permute-start.2) | collective-permute-done | bytes 131104 | tf_op jit(solution)/shard_map/ppermute | solution.py:161
  113.8 0.0 collective-permute-done
  113.8 0.1 pad_maximum_fusion
  113.8 1.0 constant_dynamic-slice_fusion
  114.8 3.1 %collective-permute-start.5 = (bf16[4,2,128,128]{3,2,1,0:T(8,128)(2,1)}, bf16[4,2,128,128]{3,2,1,0:T(8,128)(2,1)S(1)}, u32[]{:S(2)}, u32[]{:S(2)}) collective-permute-start(bf16[4,2,128,128]{3,2,1,0:T(8,128)(2,1)} %get-tuple-element.5), channel_id=1, source_target_pairs={{0,3},{1,0},{2,1},{3,2},{4,7},{5,4},{6,5},{7,6},{8,11},{9,8},{10,9... | collective-permute-start | bytes 786440 | tf_op jit(solution)/shard_map/ppermute | solution.py:169
  117.9 1.9 collective-permute-start.4
  119.8 2.8 %collective-permute-start.3 = (bf16[4,2,128,128]{3,2,1,0:T(8,128)(2,1)}, bf16[4,2,128,128]{3,2,1,0:T(8,128)(2,1)}, u32[]{:S(2)}, u32[]{:S(2)}) collective-permute-start(bf16[4,2,128,128]{3,2,1,0:T(8,128)(2,1)} %get-tuple-element.7), channel_id=1, source_target_pairs={{0,1},{1,2},{2,3},{3,0},{4,5},{5,6},{6,7},{7,4},{8,9},{9,10},{10,1... | collective-permute-start | bytes 786440 | tf_op jit(solution)/shard_map/ppermute | solution.py:169
  123.3 0.2 fusion.2
  123.5 0.1 concatenate.7.info
  123.6 2.5 collective-permute-done.5.refs_3_
  126.1 0.7 copy-done.1
  126.8 3.9 %collective-permute-done.4.refs_2_ = bf16[4,2,128,128]{3,2,1,0:T(8,128)(2,1)S(1)} collective-permute-done((bf16[4,2,128,128]{3,2,1,0:T(8,128)(2,1)}, bf16[4,2,128,128]{3,2,1,0:T(8,128)(2,1)S(1)}, u32[]{:S(2)}, u32[]{:S(2)}) %collective-permute-start.4) | collective-permute-done | bytes 262176 | tf_op jit(solution)/shard_map/ppermute | solution.py:169
  130.7 0.7 copy-done.3
  131.4 3.8 %collective-permute-done.3.refs_1_ = bf16[4,2,128,128]{3,2,1,0:T(8,128)(2,1)} collective-permute-done((bf16[4,2,128,128]{3,2,1,0:T(8,128)(2,1)}, bf16[4,2,128,128]{3,2,1,0:T(8,128)(2,1)}, u32[]{:S(2)}, u32[]{:S(2)}) %collective-permute-start.3) | collective-permute-done | bytes 262176 | tf_op jit(solution)/shard_map/ppermute | solution.py:169
  135.2 0.9 copy-done.2
  136.1 0.9 copy-done.4
  137.1 8.0 %attend.1.refs_0_ = bf16[512,512]{1,0:T(8,128)(2,1)S(1)} custom-call(s32[21]{0:T(128)S(1)} %concatenate.7.info, bf16[512,512]{1,0:T(8,128)(2,1)S(1)} %bitcast.47, bf16[4,2,128,128]{3,2,1,0:T(8,128)(2,1)S(1)} %get-tuple-element.8.refs_0_, bf16[4,2,128,128]{3,2,1,0:T(8,128)(2,1)} %collective-permute-done.3.refs_1_, bf16[4,2,128,128]{3,2,1,0:T(8,128)(2,1)S(1)} %copy-done.4, ...), custom_call_target="tpu_custom_call" | custom-call | flops 2147483648 | bytes 2097152 | tf_op jit(solution)/shard_map/attend/pallas_call | solution.py:63
  145.0 2.5 collective-permute-start.8
  147.6 2.2 collective-permute-start.7
  149.7 3.1 %collective-permute-start.6 = (bf16[512,512]{1,0:T(8,128)(2,1)S(1)}, bf16[512,512]{1,0:T(8,128)(2,1)}, u32[]{:S(2)}, u32[]{:S(2)}) collective-permute-start(bf16[512,512]{1,0:T(8,128)(2,1)S(1)} %attend.1.refs_0_), channel_id=1, source_target_pairs={{0,1},{1,2},{2,3},{3,0},{4,5},{5,6},{6,7},{7,4},{8,9},{9,10},{10,1... | collective-permute-start | bytes 1572872 | tf_op jit(solution)/shard_map/ppermute | solution.py:186
  152.8 0.1 stack.119.where
  152.9 8.8 %collective-permute-done.8.refs_3_ = bf16[512,512]{1,0:T(8,128)(2,1)S(1)} collective-permute-done((bf16[512,512]{1,0:T(8,128)(2,1)S(1)}, bf16[512,512]{1,0:T(8,128)(2,1)S(1)}, u32[]{:S(2)}, u32[]{:S(2)}) %collective-permute-start.8) | collective-permute-done | bytes 524320 | tf_op jit(solution)/shard_map/ppermute | solution.py:186
  161.7 4.2 %collective-permute-done.7.refs_2_ = bf16[512,512]{1,0:T(8,128)(2,1)} collective-permute-done((bf16[512,512]{1,0:T(8,128)(2,1)S(1)}, bf16[512,512]{1,0:T(8,128)(2,1)}, u32[]{:S(2)}, u32[]{:S(2)}) %collective-permute-start.7) | collective-permute-done | bytes 524320 | tf_op jit(solution)/shard_map/ppermute | solution.py:186
  165.9 9.6 %collective-permute-done.6.refs_1_ = bf16[512,512]{1,0:T(8,128)(2,1)} collective-permute-done((bf16[512,512]{1,0:T(8,128)(2,1)S(1)}, bf16[512,512]{1,0:T(8,128)(2,1)}, u32[]{:S(2)}, u32[]{:S(2)}) %collective-permute-start.6) | collective-permute-done | bytes 524320 | tf_op jit(solution)/shard_map/ppermute | solution.py:186
  175.5 0.0 collective-permute-done.12.refs_5_
  175.5 5.3 %project.1 = bf16[4,512,256]{2,1,0:T(8,128)(2,1)S(1)} custom-call(s32[6]{0:T(128)S(1)} %stack.119.where, bf16[512,512]{1,0:T(8,128)(2,1)S(1)} %attend.1.refs_0_, bf16[512,512]{1,0:T(8,128)(2,1)} %collective-permute-done.6.refs_1_, bf16[512,512]{1,0:T(8,128)(2,1)} %collective-permute-done.7.refs_2_, bf16[512,512]{1,0:T(8,128)(2,1)S(1)} %collective-permute-done.8.refs_3_, ...), custom_call_target="tpu_custom_call" | custom-call | flops 2147483648 | bytes 8388608 | tf_op jit(solution)/shard_map/project/pallas_call | solution.py:114
  180.8 71.1 %all_to_all.15 = bf16[128,16,256]{2,1,0:T(8,128)(2,1)S(1)} all-to-all(bf16[128,16,256]{2,1,0:T(8,128)(2,1)S(1)} %bitcast.46), channel_id=1, replica_groups=mesh['zl'=4,'y'=4,'c'=2,'zh'=4,'x'=4] {'zh','y','c','zl'}, dimensions={0} | all-to-all | bytes 2097152 | tf_op jit(solution)/shard_map/all_to_all | solution.py:191
  251.9 0.1 bitcast_reduce_fusion
  252.2 0.7 copy-done.8
  252.9 0.8 fusion
  (25 shorter events, 0.2 us)
Async XLA Ops:
  0.0 123.3 %copy-start = (s32[32,4]{0,1:T(4,128)S(1)}, s32[32,4]{0,1:T(4,128)}, u32[]{:S(2)}) copy-start(s32[32,4]{0,1:T(4,128)} %param.10) | copy-start | bytes 1540
  0.0 13.6 %collective-permute-start.9 = (bf16[512,128]{1,0:T(8,128)(2,1)}, bf16[512,128]{1,0:T(8,128)(2,1)S(1)}, u32[]{:S(2)}, u32[]{:S(2)}) collective-permute-start(bf16[512,128]{1,0:T(8,128)(2,1)} %param.14), channel_id=1, source_target_pairs={{0,0},{1,32},{2,64},{3,96},{32,1},{33,33},{34,65},{35,97},{64,2},{... | collective-permute-start | bytes 393224 | tf_op jit(solution)/shard_map/ppermute | solution.py:135
  13.6 7.0 %collective-permute-start.10 = (bf16[512,128]{1,0:T(8,128)(2,1)S(1)}, bf16[512,128]{1,0:T(8,128)(2,1)S(1)}, u32[]{:S(2)}, u32[]{:S(2)}) collective-permute-start(bf16[512,128]{1,0:T(8,128)(2,1)S(1)} %collective-permute-done.9), channel_id=1, source_target_pairs={{0,128},{128,0},{256,384},{384,256},{1,129},{129,1},{257,385},{385... | collective-permute-start | bytes 393224 | tf_op jit(solution)/shard_map/ppermute | solution.py:136
  20.6 16.1 %collective-permute-start.11 = (bf16[2,512,128]{2,1,0:T(8,128)(2,1)S(1)}, bf16[2,512,128]{2,1,0:T(8,128)(2,1)S(1)}, u32[]{:S(2)}, u32[]{:S(2)}) collective-permute-start(bf16[2,512,128]{2,1,0:T(8,128)(2,1)S(1)} %pad_maximum_fusion.2), channel_id=1, source_target_pairs={{0,256},{128,384},{256,0},{384,128},{1,257},{129,385},{257,1},{385... | collective-permute-start | bytes 786440 | tf_op jit(solution)/shard_map/ppermute | solution.py:137
  38.6 4.7 %copy-start.5 = (bf16[512,512]{1,0:T(8,128)(2,1)S(1)}, bf16[512,512]{1,0:T(8,128)(2,1)}, u32[]{:S(2)}) copy-start(bf16[512,512]{1,0:T(8,128)(2,1)} %param.8) | copy-start | bytes 1572868
  38.6 4.7 %copy-start.9 = (s32[512]{0:T(512)S(1)}, s32[512]{0:T(512)}, u32[]{:S(2)}) copy-start(s32[512]{0:T(512)} %param.9) | copy-start | bytes 6148
  38.6 28.4 %all-to-all-start.1 = ((bf16[4,4,512,128]{3,2,1,0:T(8,128)(2,1)}), bf16[4,4,512,128]{3,2,1,0:T(8,128)(2,1)S(1)}, u32[]{:S(2)}, u32[]{:S(2)}) async-start(bf16[4,4,512,128]{3,2,1,0:T(8,128)(2,1)} %broadcast_in_dim.12), calls=%async_computation.1 | async-start | bytes 4194304 | tf_op jit(solution)/shard_map/all_to_all | solution.py:139
  43.2 33.8 %copy-start.6 = (bf16[1,128,1024]{2,1,0:T(8,128)(2,1)S(1)}, bf16[1,128,1024]{2,1,0:T(8,128)(2,1)}, u32[]{:S(2)}) copy-start(bf16[1,128,1024]{2,1,0:T(8,128)(2,1)} %param.12) | copy-start | bytes 786436
  43.2 33.9 %copy-start.7 = (bf16[1,128,1024]{2,1,0:T(8,128)(2,1)S(1)}, bf16[1,128,1024]{2,1,0:T(8,128)(2,1)}, u32[]{:S(2)}) copy-start(bf16[1,128,1024]{2,1,0:T(8,128)(2,1)} %param.11) | copy-start | bytes 786436
  66.9 68.2 %all-to-all-start = ((bf16[32,16,512]{2,1,0:T(8,128)(2,1)}), bf16[32,16,512]{2,1,0:T(8,128)(2,1)S(1)}, u32[]{:S(2)}, u32[]{:S(2)}) async-start(bf16[32,16,512]{2,1,0:T(8,128)(2,1)} %bitcast.24), calls=%async_computation | async-start | bytes 1048576 | tf_op jit(solution)/shard_map/all_to_all | solution.py:177
  75.0 100.6 %collective-permute-start.12 = (bf16[4,4,512,128]{3,2,1,0:T(8,128)(2,1)S(1)}, bf16[4,4,512,128]{3,2,1,0:T(8,128)(2,1)}, u32[]{:S(2)}, u32[]{:S(2)}) collective-permute-start(bf16[4,4,512,128]{3,2,1,0:T(8,128)(2,1)S(1)} %all-to-all-done.1.refs_4_), channel_id=1, source_target_pairs={{0,16},{16,0},{1,17},{17,1},{2,18},{18,2},{3,19},{19,3},{4,20},{20... | collective-permute-start | bytes 6291464 | tf_op jit(solution)/shard_map/ppermute | solution.py:140
  77.2 22.6 %collective-permute-start.1 = (bf16[2,128,256]{2,1,0:T(8,128)(2,1)S(1)}, bf16[2,128,256]{2,1,0:T(8,128)(2,1)S(1)}, u32[]{:S(2)}, u32[]{:S(2)}) collective-permute-start(bf16[2,128,256]{2,1,0:T(8,128)(2,1)S(1)} %pad_maximum_fusion.4), channel_id=1, source_target_pairs={{0,8},{4,12},{8,0},{12,4},{1,9},{5,13},{9,1},{13,5},{2,10},{6,14},... | collective-permute-start | bytes 393224 | tf_op jit(solution)/shard_map/ppermute | solution.py:161
  90.0 23.8 %collective-permute-start.2 = (bf16[2,128,256]{2,1,0:T(8,128)(2,1)S(1)}, bf16[2,128,256]{2,1,0:T(8,128)(2,1)S(1)}, u32[]{:S(2)}, u32[]{:S(2)}) collective-permute-start(bf16[2,128,256]{2,1,0:T(8,128)(2,1)S(1)} %pad_maximum_fusion.5), channel_id=1, source_target_pairs={{0,12},{4,0},{8,4},{12,8},{1,13},{5,1},{9,5},{13,9},{2,14},{6,2},{... | collective-permute-start | bytes 393224 | tf_op jit(solution)/shard_map/ppermute | solution.py:161
  93.6 20.2 %collective-permute-start = (bf16[2,128,256]{2,1,0:T(8,128)(2,1)S(1)}, bf16[2,128,256]{2,1,0:T(8,128)(2,1)S(1)}, u32[]{:S(2)}, u32[]{:S(2)}) collective-permute-start(bf16[2,128,256]{2,1,0:T(8,128)(2,1)S(1)} %pad_maximum_fusion.3), channel_id=1, source_target_pairs={{0,4},{4,8},{8,12},{12,0},{1,5},{5,9},{9,13},{13,1},{2,6},{6,10},{... | collective-permute-start | bytes 393224 | tf_op jit(solution)/shard_map/ppermute | solution.py:161
  114.8 11.3 %collective-permute-start.5 = (bf16[4,2,128,128]{3,2,1,0:T(8,128)(2,1)}, bf16[4,2,128,128]{3,2,1,0:T(8,128)(2,1)S(1)}, u32[]{:S(2)}, u32[]{:S(2)}) collective-permute-start(bf16[4,2,128,128]{3,2,1,0:T(8,128)(2,1)} %get-tuple-element.5), channel_id=1, source_target_pairs={{0,3},{1,0},{2,1},{3,2},{4,7},{5,4},{6,5},{7,6},{8,11},{9,8},{10,9... | collective-permute-start | bytes 786440 | tf_op jit(solution)/shard_map/ppermute | solution.py:169
  117.9 12.8 %collective-permute-start.4 = (bf16[4,2,128,128]{3,2,1,0:T(8,128)(2,1)}, bf16[4,2,128,128]{3,2,1,0:T(8,128)(2,1)S(1)}, u32[]{:S(2)}, u32[]{:S(2)}) collective-permute-start(bf16[4,2,128,128]{3,2,1,0:T(8,128)(2,1)} %get-tuple-element.6), channel_id=1, source_target_pairs={{0,2},{1,3},{2,0},{3,1},{4,6},{5,7},{6,4},{7,5},{8,10},{9,11},{10,... | collective-permute-start | bytes 786440 | tf_op jit(solution)/shard_map/ppermute | solution.py:169
  119.8 15.4 %collective-permute-start.3 = (bf16[4,2,128,128]{3,2,1,0:T(8,128)(2,1)}, bf16[4,2,128,128]{3,2,1,0:T(8,128)(2,1)}, u32[]{:S(2)}, u32[]{:S(2)}) collective-permute-start(bf16[4,2,128,128]{3,2,1,0:T(8,128)(2,1)} %get-tuple-element.7), channel_id=1, source_target_pairs={{0,1},{1,2},{2,3},{3,0},{4,5},{5,6},{6,7},{7,4},{8,9},{9,10},{10,1... | collective-permute-start | bytes 786440 | tf_op jit(solution)/shard_map/ppermute | solution.py:169
  126.1 0.7 copy-start.1
  130.7 0.7 copy-start.3
  135.2 1.0 copy-start.2
  136.1 0.9 copy-start.4
  145.0 16.7 %collective-permute-start.8 = (bf16[512,512]{1,0:T(8,128)(2,1)S(1)}, bf16[512,512]{1,0:T(8,128)(2,1)S(1)}, u32[]{:S(2)}, u32[]{:S(2)}) collective-permute-start(bf16[512,512]{1,0:T(8,128)(2,1)S(1)} %attend.1.refs_0_), channel_id=1, source_target_pairs={{0,3},{1,0},{2,1},{3,2},{4,7},{5,4},{6,5},{7,6},{8,11},{9,8},{10,9... | collective-permute-start | bytes 1572872 | tf_op jit(solution)/shard_map/ppermute | solution.py:186
  147.6 18.3 %collective-permute-start.7 = (bf16[512,512]{1,0:T(8,128)(2,1)S(1)}, bf16[512,512]{1,0:T(8,128)(2,1)}, u32[]{:S(2)}, u32[]{:S(2)}) collective-permute-start(bf16[512,512]{1,0:T(8,128)(2,1)S(1)} %attend.1.refs_0_), channel_id=1, source_target_pairs={{0,2},{1,3},{2,0},{3,1},{4,6},{5,7},{6,4},{7,5},{8,10},{9,11},{10,... | collective-permute-start | bytes 1572872 | tf_op jit(solution)/shard_map/ppermute | solution.py:186
  149.7 25.8 %collective-permute-start.6 = (bf16[512,512]{1,0:T(8,128)(2,1)S(1)}, bf16[512,512]{1,0:T(8,128)(2,1)}, u32[]{:S(2)}, u32[]{:S(2)}) collective-permute-start(bf16[512,512]{1,0:T(8,128)(2,1)S(1)} %attend.1.refs_0_), channel_id=1, source_target_pairs={{0,1},{1,2},{2,3},{3,0},{4,5},{5,6},{6,7},{7,4},{8,9},{9,10},{10,1... | collective-permute-start | bytes 1572872 | tf_op jit(solution)/shard_map/ppermute | solution.py:186
  251.9 1.0 copy-start.8

commit v4 on v3

--- a/solution.py
+++ b/solution.py
@@ -189,10 +189,11 @@
     partial = project(where, gathered, own, other)
     partial = partial.reshape(4 * prompts, per_prompt, 256)
     returned = lax.all_to_all(partial, ("zh", "y", "c", "zl"), 0, 0, tiled=True)
-    projected = jnp.sum(returned.reshape(4, row_count, 256).astype(jnp.float32), axis=0)
-    projected = projected.astype(jnp.bfloat16).reshape(prompts // 4, 4, per_prompt, 256)
-    projected = projected.transpose(1, 0, 2, 3).reshape(row_count, 256)
-    return (residual.astype(jnp.float32) + projected.astype(jnp.float32)).astype(jnp.bfloat16)
+    returned = returned.reshape(4, prompts // 4, 4, per_prompt, 256).astype(jnp.float32)
+    projected = jnp.sum(returned, axis=0).astype(jnp.bfloat16).astype(jnp.float32)
+    before = residual.reshape(4, prompts // 4, per_prompt, 256).astype(jnp.float32)
+    patched = [(before[z] + projected[:, z]).astype(jnp.bfloat16) for z in range(4)]
+    return jnp.concatenate(patched, axis=0).reshape(row_count, 256)
 
 
 def solution(mesh):

time: 255 us -> 257 us (level)
  blocking collectives: 71.1 us -> 0 us
  waiting for transfers between devices: 92.7 us -> 148 us
  starting transfers between devices: 66.2 us -> 85.5 us
    all_to_all x1 -> x0, blocking collectives: 71.1 us -> none  [step(): returned = lax.all_to_all(partial, ('zh', 'y', 'c', 'zl'), 0, 0, tiled=True)]
    all_to_all x0 -> x1, waiting for transfers between devices: none -> 56.3 us  [step(): returned = lax.all_to_all(partial, ('zh', 'y', 'c', 'zl'), 0, 0, tiled=True)]
    all_to_all x0 -> x1, starting transfers between devices: none -> 16.1 us  [step(): returned = lax.all_to_all(partial, ('zh', 'y', 'c', 'zl'), 0, 0, tiled=True)]
    ppermute x3, waiting for transfers between devices: 14 us -> 16.9 us  [step(): kv.append(lax.ppermute(heads_for(zh + s & 3), 'zh', shifted(4, s)))]
  transfers between devices with their start and end apart: 15 -> 16, of which waited for: 11 -> 12; matrix products, arithmetic and copies ran while one was open for 1% -> 1% of each run, Pallas kernels for 3% -> 3%
where the time goes in v4:
time: 257 us
  waiting for transfers between devices  148 us (58%)
  starting transfers between devices  85.5 us (33%)
  Pallas kernels  13 us (5%)
  local copies, waits for them, and re-layouts  7.39 us (3%)
    all_to_all x1, waiting for transfers between devices, step(): returned = lax.all_to_all(partial, ('zh', 'y', 'c', 'zl'), 0, 0, tiled=True)  56.3 us
    all_to_all x1, waiting for transfers between devices, gather_weight(): lax.all_to_all(jnp.broadcast_to(along[None], (4,) + along.shape), 'y', 0,...  22.6 us
    ppermute x3, starting transfers between devices, step(): kv.append(lax.ppermute(heads_for(zh + s & 3), 'zh', shifted(4, s)))  22.5 us
    ppermute x3, waiting for transfers between devices, step(): gathered.append(lax.ppermute(gated, 'x', shifted(4, s)))  20.6 us
    ppermute x3, waiting for transfers between devices, step(): kv.append(lax.ppermute(heads_for(zh + s & 3), 'zh', shifted(4, s)))  16.9 us
    all_to_all x1, starting transfers between devices, step(): returned = lax.all_to_all(partial, ('zh', 'y', 'c', 'zl'), 0, 0, tiled=True)  16.1 us
    ppermute x1, waiting for transfers between devices, gather_weight(): far = lax.ppermute(pair, 'zl', [(i, i ^ 2) for i in range(4)])  10.9 us
    ppermute x3, starting transfers between devices, step(): gathered.append(lax.ppermute(gated, 'x', shifted(4, s)))  9.83 us
  transfers between devices with their start and end apart: 16, of which 12 were waited for; matrix products, arithmetic and copies ran while one was open for 1% of the time, Pallas kernels for 3%

profile of v4, /device:TPU:24, one launch (start us, length us, event | category | flops | bytes accessed | tf_op | source)
XLA Modules:
  0.0 256.6 jit_solution(15782912758573668784)
XLA Ops:
  0.0 4.4 %collective-permute-start.9 = (bf16[512,128]{1,0:T(8,128)(2,1)}, bf16[512,128]{1,0:T(8,128)(2,1)S(1)}, u32[]{:S(2)}, u32[]{:S(2)}) collective-permute-start(bf16[512,128]{1,0:T(8,128)(2,1)} %param.14), channel_id=1, source_target_pairs={{0,0},{1,32},{2,64},{3,96},{32,1},{33,33},{34,65},{35,97},{64,2},{... | collective-permute-start | bytes 393224 | tf_op jit(solution)/shard_map/ppermute | solution.py:135
  4.5 9.1 %collective-permute-done.9 = bf16[512,128]{1,0:T(8,128)(2,1)S(1)} collective-permute-done((bf16[512,128]{1,0:T(8,128)(2,1)}, bf16[512,128]{1,0:T(8,128)(2,1)S(1)}, u32[]{:S(2)}, u32[]{:S(2)}) %collective-permute-start.9) | collective-permute-done | bytes 131104 | tf_op jit(solution)/shard_map/ppermute | solution.py:135
  13.6 3.8 %collective-permute-start.10 = (bf16[512,128]{1,0:T(8,128)(2,1)S(1)}, bf16[512,128]{1,0:T(8,128)(2,1)S(1)}, u32[]{:S(2)}, u32[]{:S(2)}) collective-permute-start(bf16[512,128]{1,0:T(8,128)(2,1)S(1)} %collective-permute-done.9), channel_id=1, source_target_pairs={{0,128},{128,0},{256,384},{384,256},{1,129},{129,1},{257,385},{385... | collective-permute-start | bytes 393224 | tf_op jit(solution)/shard_map/ppermute | solution.py:136
  17.4 3.2 %collective-permute-done.10 = bf16[512,128]{1,0:T(8,128)(2,1)S(1)} collective-permute-done((bf16[512,128]{1,0:T(8,128)(2,1)S(1)}, bf16[512,128]{1,0:T(8,128)(2,1)S(1)}, u32[]{:S(2)}, u32[]{:S(2)}) %collective-permute-start.10) | collective-permute-done | bytes 131104 | tf_op jit(solution)/shard_map/ppermute | solution.py:136
  20.6 5.2 %collective-permute-start.11 = (bf16[2,512,128]{2,1,0:T(8,128)(2,1)S(1)}, bf16[2,512,128]{2,1,0:T(8,128)(2,1)S(1)}, u32[]{:S(2)}, u32[]{:S(2)}) collective-permute-start(bf16[2,512,128]{2,1,0:T(8,128)(2,1)S(1)} %pad_maximum_fusion.2), channel_id=1, source_target_pairs={{0,256},{128,384},{256,0},{384,128},{1,257},{129,385},{257,1},{385... | collective-permute-start | bytes 786440 | tf_op jit(solution)/shard_map/ppermute | solution.py:137
  25.8 10.9 %collective-permute-done.11 = bf16[2,512,128]{2,1,0:T(8,128)(2,1)S(1)} collective-permute-done((bf16[2,512,128]{2,1,0:T(8,128)(2,1)S(1)}, bf16[2,512,128]{2,1,0:T(8,128)(2,1)S(1)}, u32[]{:S(2)}, u32[]{:S(2)}) %collective-permute-start.11) | collective-permute-done | bytes 262176 | tf_op jit(solution)/shard_map/ppermute | solution.py:137
  36.8 0.1 pad_maximum_fusion.1
  36.8 1.7 broadcast_in_dim.12
  38.6 4.6 %all-to-all-start.1 = ((bf16[4,4,512,128]{3,2,1,0:T(8,128)(2,1)}), bf16[4,4,512,128]{3,2,1,0:T(8,128)(2,1)S(1)}, u32[]{:S(2)}, u32[]{:S(2)}) async-start(bf16[4,4,512,128]{3,2,1,0:T(8,128)(2,1)} %broadcast_in_dim.12), calls=%async_computation.1 | async-start | bytes 4194304 | tf_op jit(solution)/shard_map/all_to_all | solution.py:139
  43.2 0.2 compare_select_fusion
  43.4 0.9 copy.10
  44.3 22.6 %all-to-all-done.1.refs_4_ = bf16[4,4,512,128]{3,2,1,0:T(8,128)(2,1)S(1)} async-done(((bf16[4,4,512,128]{3,2,1,0:T(8,128)(2,1)}), bf16[4,4,512,128]{3,2,1,0:T(8,128)(2,1)S(1)}, u32[]{:S(2)}, u32[]{:S(2)}) %all-to-all-start.1) | async-done | bytes 2097184 | tf_op jit(solution)/shard_map/all_to_all | solution.py:139
  66.9 8.0 %all-to-all-start = ((bf16[32,16,512]{2,1,0:T(8,128)(2,1)}), bf16[32,16,512]{2,1,0:T(8,128)(2,1)S(1)}, u32[]{:S(2)}, u32[]{:S(2)}) async-start(bf16[32,16,512]{2,1,0:T(8,128)(2,1)} %bitcast.25), calls=%async_computation | async-start | bytes 1048576 | tf_op jit(solution)/shard_map/all_to_all | solution.py:177
  75.0 2.1 collective-permute-start.12
  77.1 0.1 constant_dynamic-slice_fusion.10
  77.2 9.1 %collective-permute-start = (bf16[2,128,256]{2,1,0:T(8,128)(2,1)S(1)}, bf16[2,128,256]{2,1,0:T(8,128)(2,1)S(1)}, u32[]{:S(2)}, u32[]{:S(2)}) collective-permute-start(bf16[2,128,256]{2,1,0:T(8,128)(2,1)S(1)} %pad_maximum_fusion.4), channel_id=1, source_target_pairs={{0,4},{4,8},{8,12},{12,0},{1,5},{5,9},{9,13},{13,1},{2,6},{6,10},{... | collective-permute-start | bytes 393224 | tf_op jit(solution)/shard_map/ppermute | solution.py:161
  86.3 8.0 %collective-permute-start.1 = (bf16[2,128,256]{2,1,0:T(8,128)(2,1)S(1)}, bf16[2,128,256]{2,1,0:T(8,128)(2,1)S(1)}, u32[]{:S(2)}, u32[]{:S(2)}) collective-permute-start(bf16[2,128,256]{2,1,0:T(8,128)(2,1)S(1)} %pad_maximum_fusion.5), channel_id=1, source_target_pairs={{0,8},{4,12},{8,0},{12,4},{1,9},{5,13},{9,1},{13,5},{2,10},{6,14},... | collective-permute-start | bytes 393224 | tf_op jit(solution)/shard_map/ppermute | solution.py:161
  94.3 5.5 %collective-permute-start.2 = (bf16[2,128,256]{2,1,0:T(8,128)(2,1)S(1)}, bf16[2,128,256]{2,1,0:T(8,128)(2,1)S(1)}, u32[]{:S(2)}, u32[]{:S(2)}) collective-permute-start(bf16[2,128,256]{2,1,0:T(8,128)(2,1)S(1)} %pad_maximum_fusion.6), channel_id=1, source_target_pairs={{0,12},{4,0},{8,4},{12,8},{1,13},{5,1},{9,5},{13,9},{2,14},{6,2},{... | collective-permute-start | bytes 393224 | tf_op jit(solution)/shard_map/ppermute | solution.py:161
  99.8 7.7 %collective-permute-done.1 = bf16[2,128,256]{2,1,0:T(8,128)(2,1)S(1)} collective-permute-done((bf16[2,128,256]{2,1,0:T(8,128)(2,1)S(1)}, bf16[2,128,256]{2,1,0:T(8,128)(2,1)S(1)}, u32[]{:S(2)}, u32[]{:S(2)}) %collective-permute-start.1) | collective-permute-done | bytes 131104 | tf_op jit(solution)/shard_map/ppermute | solution.py:161
  107.5 9.2 %collective-permute-done.2 = bf16[2,128,256]{2,1,0:T(8,128)(2,1)S(1)} collective-permute-done((bf16[2,128,256]{2,1,0:T(8,128)(2,1)S(1)}, bf16[2,128,256]{2,1,0:T(8,128)(2,1)S(1)}, u32[]{:S(2)}, u32[]{:S(2)}) %collective-permute-start.2) | collective-permute-done | bytes 131104 | tf_op jit(solution)/shard_map/ppermute | solution.py:161
  116.7 0.1 pad_maximum_fusion
  116.7 1.0 constant_dynamic-slice_fusion
  117.7 1.9 collective-permute-start.3
  119.6 4.8 %collective-permute-start.4 = (bf16[4,2,128,128]{3,2,1,0:T(8,128)(2,1)}, bf16[4,2,128,128]{3,2,1,0:T(8,128)(2,1)S(1)}, u32[]{:S(2)}, u32[]{:S(2)}) collective-permute-start(bf16[4,2,128,128]{3,2,1,0:T(8,128)(2,1)} %get-tuple-element.10), channel_id=1, source_target_pairs={{0,2},{1,3},{2,0},{3,1},{4,6},{5,7},{6,4},{7,5},{8,10},{9,11},{10,... | collective-permute-start | bytes 786440 | tf_op jit(solution)/shard_map/ppermute | solution.py:169
  124.5 2.2 collective-permute-start.5
  127.4 0.2 fusion.9
  127.6 0.1 concatenate.10.info
  127.7 7.2 %collective-permute-done.3.refs_1_ = bf16[4,2,128,128]{3,2,1,0:T(8,128)(2,1)S(1)} collective-permute-done((bf16[4,2,128,128]{3,2,1,0:T(8,128)(2,1)}, bf16[4,2,128,128]{3,2,1,0:T(8,128)(2,1)S(1)}, u32[]{:S(2)}, u32[]{:S(2)}) %collective-permute-start.3) | collective-permute-done | bytes 262176 | tf_op jit(solution)/shard_map/ppermute | solution.py:169
  134.9 0.7 copy-done.1
  135.6 0.7 copy-done.3
  136.3 1.2 collective-permute-done.5.refs_3_
  137.5 0.9 copy-done.2
  138.5 0.9 copy-done.4
  139.4 7.9 %attend.1.refs_0_ = bf16[512,512]{1,0:T(8,128)(2,1)S(1)} custom-call(s32[21]{0:T(128)S(1)} %concatenate.10.info, bf16[512,512]{1,0:T(8,128)(2,1)S(1)} %bitcast.71, bf16[4,2,128,128]{3,2,1,0:T(8,128)(2,1)S(1)} %get-tuple-element.12.refs_0_, bf16[4,2,128,128]{3,2,1,0:T(8,128)(2,1)S(1)} %copy-done.2, bf16[4,2,128,128]{3,2,1,0:T(8,128)(2,1)S(1)} %copy-done.4, ...), custom_call_target="tpu_custom_call" | custom-call | flops 2147483648 | bytes 2097152 | tf_op jit(solution)/shard_map/attend/pallas_call | solution.py:63
  147.4 2.2 collective-permute-start.6
  149.5 5.7 %collective-permute-start.7 = (bf16[512,512]{1,0:T(8,128)(2,1)S(1)}, bf16[512,512]{1,0:T(8,128)(2,1)}, u32[]{:S(2)}, u32[]{:S(2)}) collective-permute-start(bf16[512,512]{1,0:T(8,128)(2,1)S(1)} %attend.1.refs_0_), channel_id=1, source_target_pairs={{0,2},{1,3},{2,0},{3,1},{4,6},{5,7},{6,4},{7,5},{8,10},{9,11},{10,... | collective-permute-start | bytes 1572872 | tf_op jit(solution)/shard_map/ppermute | solution.py:186
  155.3 1.9 collective-permute-start.8
  157.2 0.1 stack.119.where
  157.3 6.7 %collective-permute-done.6.refs_1_ = bf16[512,512]{1,0:T(8,128)(2,1)S(1)} collective-permute-done((bf16[512,512]{1,0:T(8,128)(2,1)S(1)}, bf16[512,512]{1,0:T(8,128)(2,1)S(1)}, u32[]{:S(2)}, u32[]{:S(2)}) %collective-permute-start.6) | collective-permute-done | bytes 524320 | tf_op jit(solution)/shard_map/ppermute | solution.py:186
  164.0 12.5 %collective-permute-done.7.refs_2_ = bf16[512,512]{1,0:T(8,128)(2,1)} collective-permute-done((bf16[512,512]{1,0:T(8,128)(2,1)S(1)}, bf16[512,512]{1,0:T(8,128)(2,1)}, u32[]{:S(2)}, u32[]{:S(2)}) %collective-permute-start.7) | collective-permute-done | bytes 524320 | tf_op jit(solution)/shard_map/ppermute | solution.py:186
  176.5 1.4 collective-permute-done.8.refs_3_
  177.9 5.1 %project.1 = bf16[4,512,256]{2,1,0:T(8,128)(2,1)} custom-call(s32[6]{0:T(128)S(1)} %stack.119.where, bf16[512,512]{1,0:T(8,128)(2,1)S(1)} %attend.1.refs_0_, bf16[512,512]{1,0:T(8,128)(2,1)S(1)} %collective-permute-done.6.refs_1_, bf16[512,512]{1,0:T(8,128)(2,1)} %collective-permute-done.7.refs_2_, bf16[512,512]{1,0:T(8,128)(2,1)} %collective-permute-done.8.refs_3_, ...), custom_call_target="tpu_custom_call" | custom-call | flops 2147483648 | bytes 8388608 | tf_op jit(solution)/shard_map/project/pallas_call | solution.py:114
  183.0 0.0 copy-start.5
  183.0 16.1 %all-to-all-start.2 = ((bf16[128,16,256]{2,1,0:T(8,128)(2,1)}), bf16[128,16,256]{2,1,0:T(8,128)(2,1)S(1)}, u32[]{:S(2)}, u32[]{:S(2)}) async-start(bf16[128,16,256]{2,1,0:T(8,128)(2,1)} %bitcast.33), calls=%async_computation.2 | async-start | bytes 2097152 | tf_op jit(solution)/shard_map/all_to_all | solution.py:191
  199.1 56.3 %all-to-all-done.2 = bf16[128,16,256]{2,1,0:T(8,128)(2,1)S(1)} async-done(((bf16[128,16,256]{2,1,0:T(8,128)(2,1)}), bf16[128,16,256]{2,1,0:T(8,128)(2,1)S(1)}, u32[]{:S(2)}, u32[]{:S(2)}) %all-to-all-start.2) | async-done | bytes 1048608 | tf_op jit(solution)/shard_map/all_to_all | solution.py:191
  255.4 0.2 reduce_sum.12
  255.7 0.1 fusion.7
  255.8 0.7 pad_maximum_fusion.3
  (27 shorter events, 0.2 us)
Async XLA Ops:
  0.0 127.4 %copy-start = (s32[32,4]{0,1:T(4,128)S(1)}, s32[32,4]{0,1:T(4,128)}, u32[]{:S(2)}) copy-start(s32[32,4]{0,1:T(4,128)} %param.10) | copy-start | bytes 1540
  0.0 13.6 %collective-permute-start.9 = (bf16[512,128]{1,0:T(8,128)(2,1)}, bf16[512,128]{1,0:T(8,128)(2,1)S(1)}, u32[]{:S(2)}, u32[]{:S(2)}) collective-permute-start(bf16[512,128]{1,0:T(8,128)(2,1)} %param.14), channel_id=1, source_target_pairs={{0,0},{1,32},{2,64},{3,96},{32,1},{33,33},{34,65},{35,97},{64,2},{... | collective-permute-start | bytes 393224 | tf_op jit(solution)/shard_map/ppermute | solution.py:135
  13.6 7.0 %collective-permute-start.10 = (bf16[512,128]{1,0:T(8,128)(2,1)S(1)}, bf16[512,128]{1,0:T(8,128)(2,1)S(1)}, u32[]{:S(2)}, u32[]{:S(2)}) collective-permute-start(bf16[512,128]{1,0:T(8,128)(2,1)S(1)} %collective-permute-done.9), channel_id=1, source_target_pairs={{0,128},{128,0},{256,384},{384,256},{1,129},{129,1},{257,385},{385... | collective-permute-start | bytes 393224 | tf_op jit(solution)/shard_map/ppermute | solution.py:136
  20.6 16.1 %collective-permute-start.11 = (bf16[2,512,128]{2,1,0:T(8,128)(2,1)S(1)}, bf16[2,512,128]{2,1,0:T(8,128)(2,1)S(1)}, u32[]{:S(2)}, u32[]{:S(2)}) collective-permute-start(bf16[2,512,128]{2,1,0:T(8,128)(2,1)S(1)} %pad_maximum_fusion.2), channel_id=1, source_target_pairs={{0,256},{128,384},{256,0},{384,128},{1,257},{129,385},{257,1},{385... | collective-permute-start | bytes 786440 | tf_op jit(solution)/shard_map/ppermute | solution.py:137
  38.5 4.7 %copy-start.6 = (bf16[512,512]{1,0:T(8,128)(2,1)S(1)}, bf16[512,512]{1,0:T(8,128)(2,1)}, u32[]{:S(2)}) copy-start(bf16[512,512]{1,0:T(8,128)(2,1)} %param.8) | copy-start | bytes 1572868
  38.6 4.7 %copy-start.9 = (s32[512]{0:T(512)S(1)}, s32[512]{0:T(512)}, u32[]{:S(2)}) copy-start(s32[512]{0:T(512)} %param.9) | copy-start | bytes 6148
  38.6 28.4 %all-to-all-start.1 = ((bf16[4,4,512,128]{3,2,1,0:T(8,128)(2,1)}), bf16[4,4,512,128]{3,2,1,0:T(8,128)(2,1)S(1)}, u32[]{:S(2)}, u32[]{:S(2)}) async-start(bf16[4,4,512,128]{3,2,1,0:T(8,128)(2,1)} %broadcast_in_dim.12), calls=%async_computation.1 | async-start | bytes 4194304 | tf_op jit(solution)/shard_map/all_to_all | solution.py:139
  43.2 33.8 %copy-start.7 = (bf16[1,128,1024]{2,1,0:T(8,128)(2,1)S(1)}, bf16[1,128,1024]{2,1,0:T(8,128)(2,1)}, u32[]{:S(2)}) copy-start(bf16[1,128,1024]{2,1,0:T(8,128)(2,1)} %param.12) | copy-start | bytes 786436
  43.2 33.9 %copy-start.8 = (bf16[1,128,1024]{2,1,0:T(8,128)(2,1)S(1)}, bf16[1,128,1024]{2,1,0:T(8,128)(2,1)}, u32[]{:S(2)}) copy-start(bf16[1,128,1024]{2,1,0:T(8,128)(2,1)} %param.11) | copy-start | bytes 786436
  66.9 70.6 %all-to-all-start = ((bf16[32,16,512]{2,1,0:T(8,128)(2,1)}), bf16[32,16,512]{2,1,0:T(8,128)(2,1)S(1)}, u32[]{:S(2)}, u32[]{:S(2)}) async-start(bf16[32,16,512]{2,1,0:T(8,128)(2,1)} %bitcast.25), calls=%async_computation | async-start | bytes 1048576 | tf_op jit(solution)/shard_map/all_to_all | solution.py:177
  75.0 102.9 %collective-permute-start.12 = (bf16[4,4,512,128]{3,2,1,0:T(8,128)(2,1)S(1)}, bf16[4,4,512,128]{3,2,1,0:T(8,128)(2,1)}, u32[]{:S(2)}, u32[]{:S(2)}) collective-permute-start(bf16[4,4,512,128]{3,2,1,0:T(8,128)(2,1)S(1)} %all-to-all-done.1.refs_4_), channel_id=1, source_target_pairs={{0,16},{16,0},{1,17},{17,1},{2,18},{18,2},{3,19},{19,3},{4,20},{20... | collective-permute-start | bytes 6291464 | tf_op jit(solution)/shard_map/ppermute | solution.py:140
  77.2 22.6 %collective-permute-start = (bf16[2,128,256]{2,1,0:T(8,128)(2,1)S(1)}, bf16[2,128,256]{2,1,0:T(8,128)(2,1)S(1)}, u32[]{:S(2)}, u32[]{:S(2)}) collective-permute-start(bf16[2,128,256]{2,1,0:T(8,128)(2,1)S(1)} %pad_maximum_fusion.4), channel_id=1, source_target_pairs={{0,4},{4,8},{8,12},{12,0},{1,5},{5,9},{9,13},{13,1},{2,6},{6,10},{... | collective-permute-start | bytes 393224 | tf_op jit(solution)/shard_map/ppermute | solution.py:161
  86.3 21.2 %collective-permute-start.1 = (bf16[2,128,256]{2,1,0:T(8,128)(2,1)S(1)}, bf16[2,128,256]{2,1,0:T(8,128)(2,1)S(1)}, u32[]{:S(2)}, u32[]{:S(2)}) collective-permute-start(bf16[2,128,256]{2,1,0:T(8,128)(2,1)S(1)} %pad_maximum_fusion.5), channel_id=1, source_target_pairs={{0,8},{4,12},{8,0},{12,4},{1,9},{5,13},{9,1},{13,5},{2,10},{6,14},... | collective-permute-start | bytes 393224 | tf_op jit(solution)/shard_map/ppermute | solution.py:161
  94.3 22.4 %collective-permute-start.2 = (bf16[2,128,256]{2,1,0:T(8,128)(2,1)S(1)}, bf16[2,128,256]{2,1,0:T(8,128)(2,1)S(1)}, u32[]{:S(2)}, u32[]{:S(2)}) collective-permute-start(bf16[2,128,256]{2,1,0:T(8,128)(2,1)S(1)} %pad_maximum_fusion.6), channel_id=1, source_target_pairs={{0,12},{4,0},{8,4},{12,8},{1,13},{5,1},{9,5},{13,9},{2,14},{6,2},{... | collective-permute-start | bytes 393224 | tf_op jit(solution)/shard_map/ppermute | solution.py:161
  117.7 17.1 %collective-permute-start.3 = (bf16[4,2,128,128]{3,2,1,0:T(8,128)(2,1)}, bf16[4,2,128,128]{3,2,1,0:T(8,128)(2,1)S(1)}, u32[]{:S(2)}, u32[]{:S(2)}) collective-permute-start(bf16[4,2,128,128]{3,2,1,0:T(8,128)(2,1)} %get-tuple-element.11), channel_id=1, source_target_pairs={{0,1},{1,2},{2,3},{3,0},{4,5},{5,6},{6,7},{7,4},{8,9},{9,10},{10,1... | collective-permute-start | bytes 786440 | tf_op jit(solution)/shard_map/ppermute | solution.py:169
  119.6 15.9 %collective-permute-start.4 = (bf16[4,2,128,128]{3,2,1,0:T(8,128)(2,1)}, bf16[4,2,128,128]{3,2,1,0:T(8,128)(2,1)S(1)}, u32[]{:S(2)}, u32[]{:S(2)}) collective-permute-start(bf16[4,2,128,128]{3,2,1,0:T(8,128)(2,1)} %get-tuple-element.10), channel_id=1, source_target_pairs={{0,2},{1,3},{2,0},{3,1},{4,6},{5,7},{6,4},{7,5},{8,10},{9,11},{10,... | collective-permute-start | bytes 786440 | tf_op jit(solution)/shard_map/ppermute | solution.py:169
  124.5 13.0 %collective-permute-start.5 = (bf16[4,2,128,128]{3,2,1,0:T(8,128)(2,1)}, bf16[4,2,128,128]{3,2,1,0:T(8,128)(2,1)}, u32[]{:S(2)}, u32[]{:S(2)}) collective-permute-start(bf16[4,2,128,128]{3,2,1,0:T(8,128)(2,1)} %get-tuple-element.9), channel_id=1, source_target_pairs={{0,3},{1,0},{2,1},{3,2},{4,7},{5,4},{6,5},{7,6},{8,11},{9,8},{10,9... | collective-permute-start | bytes 786440 | tf_op jit(solution)/shard_map/ppermute | solution.py:169
  134.9 0.7 copy-start.1
  135.6 0.7 copy-start.3
  137.5 1.0 copy-start.2
  138.5 0.9 copy-start.4
  147.4 16.6 %collective-permute-start.6 = (bf16[512,512]{1,0:T(8,128)(2,1)S(1)}, bf16[512,512]{1,0:T(8,128)(2,1)S(1)}, u32[]{:S(2)}, u32[]{:S(2)}) collective-permute-start(bf16[512,512]{1,0:T(8,128)(2,1)S(1)} %attend.1.refs_0_), channel_id=1, source_target_pairs={{0,1},{1,2},{2,3},{3,0},{4,5},{5,6},{6,7},{7,4},{8,9},{9,10},{10,1... | collective-permute-start | bytes 1572872 | tf_op jit(solution)/shard_map/ppermute | solution.py:186
  149.5 27.0 %collective-permute-start.7 = (bf16[512,512]{1,0:T(8,128)(2,1)S(1)}, bf16[512,512]{1,0:T(8,128)(2,1)}, u32[]{:S(2)}, u32[]{:S(2)}) collective-permute-start(bf16[512,512]{1,0:T(8,128)(2,1)S(1)} %attend.1.refs_0_), channel_id=1, source_target_pairs={{0,2},{1,3},{2,0},{3,1},{4,6},{5,7},{6,4},{7,5},{8,10},{9,11},{10,... | collective-permute-start | bytes 1572872 | tf_op jit(solution)/shard_map/ppermute | solution.py:186
  155.3 22.6 %collective-permute-start.8 = (bf16[512,512]{1,0:T(8,128)(2,1)S(1)}, bf16[512,512]{1,0:T(8,128)(2,1)}, u32[]{:S(2)}, u32[]{:S(2)}) collective-permute-start(bf16[512,512]{1,0:T(8,128)(2,1)S(1)} %attend.1.refs_0_), channel_id=1, source_target_pairs={{0,3},{1,0},{2,1},{3,2},{4,7},{5,4},{6,5},{7,6},{8,11},{9,8},{10,9... | collective-permute-start | bytes 1572872 | tf_op jit(solution)/shard_map/ppermute | solution.py:186
  183.0 16.1 %copy-start.5 = (bf16[512,256]{1,0:T(8,128)(2,1)S(1)}, bf16[512,256]{1,0:T(8,128)(2,1)}, u32[]{:S(2)}) copy-start(bf16[512,256]{1,0:T(8,128)(2,1)} %param.15) | copy-start | bytes 786436
  183.0 72.5 %all-to-all-start.2 = ((bf16[128,16,256]{2,1,0:T(8,128)(2,1)}), bf16[128,16,256]{2,1,0:T(8,128)(2,1)S(1)}, u32[]{:S(2)}, u32[]{:S(2)}) async-start(bf16[128,16,256]{2,1,0:T(8,128)(2,1)} %bitcast.33), calls=%async_computation.2 | async-start | bytes 2097152 | tf_op jit(solution)/shard_map/all_to_all | solution.py:191
